TPU v7x, 256 devices: a whole 4x4x8 slice. The times are simulated.
256 devices in a mesh: depth: 32 (over z, x_hi, core), shot: 8 (over y, x_lo).
Axes of the slice: x: 4 (x_hi: 2, x_lo: 2; x = x_hi * 2 + x_lo), y: 4, z: 8, core: 2. Of those that a mesh axis runs over, the one named last changes fastest.
Arguments:
- courant: float32 [512, 64, 128], P('depth'), may hold values from 0.04 to 0.2
- wave_before: float32 [8, 512, 64, 128], P('shot', 'depth'), may hold values from -10 to 10
- wave_current: float32 [8, 512, 64, 128], P('shot', 'depth'), may hold values from -10 to 10
- adjoint_after: float32 [8, 512, 64, 128], P('shot', 'depth'), may hold values from -10 to 10
- adjoint_current: float32 [8, 512, 64, 128], P('shot', 'depth'), may hold values from -10 to 10
- source_cell: int32 [8], P('shot'), may hold values from 0 to 4194303
- wavelet: float32 [8, 4], P('shot'), may hold values from -15 to 15
- receiver_cell: int32 [8, 256], P('shot'), may hold values from 0 to 4194303
- residual: float32 [8, 4, 256], P('shot'), may hold values from -12 to 12
- history: float32 [2, 5, 512, 64, 128], P(None, None, 'depth', 'shot'), may hold values from -23 to 23, as said below
Outputs:
- gradient: float32 [512, 64, 128], P('depth', 'shot')
- direction: float32 [512, 64, 128], P('depth', 'shot')
- courant_next: float32 [512, 64, 128], P('depth')
Inputs may be any that keep to these rules, and one draw needn't show every extreme that they name: In every pair the sum over all cells of history[0] times history[1] is positive.
All inputs are finite; a program needn't handle non-finite values.
Results may differ from a plain program's by a relative error of at most 0.00026.
Values sent between devices are 32-bit elements; how exact they have to be, the bound alone decides.
A program may use at most 128 MiB of HBM per device.

v0:
```python
import jax
import jax.numpy as jnp
from jax import lax
from jax.sharding import PartitionSpec as P

STEPS = 4
PAIRS = 5


coefficients = (-205.0 / 72.0, 8.0 / 5.0, -1.0 / 5.0, 8.0 / 315.0, -1.0 / 560.0)


def with_halo(cells, sides, width):
    for axis, dim in sides:
        count = lax.axis_size(axis)
        ends = count - 1
        head = lax.slice_in_dim(cells, 0, width, axis=dim)
        tail = lax.slice_in_dim(cells, cells.shape[dim] - width, cells.shape[dim], axis=dim)
        cells = jnp.concatenate(
            [
                lax.ppermute(tail, axis, [(i, (i + 1) % count) for i in range(ends)]),
                cells,
                lax.ppermute(head, axis, [((i + 1) % count, i) for i in range(ends)]),
            ],
            axis=dim,
        )
    return cells


def laplace_core(extended):
    interior = extended[4:-4]
    count_rows = interior.shape[0]
    width_x = interior.shape[1]
    width_y = interior.shape[2]
    padded = jnp.pad(interior, ((0, 0), (4, 4), (4, 4)))
    summed = 3.0 * coefficients[0] * interior
    for reach in range(1, 5):
        weight = coefficients[reach]
        summed = summed + weight * (
            extended[4 + reach : 4 + reach + count_rows]
            + extended[4 - reach : 4 - reach + count_rows]
        )
        summed = summed + weight * (
            padded[:, 4 + reach : 4 + reach + width_x, 4 : 4 + width_y]
            + padded[:, 4 - reach : 4 - reach + width_x, 4 : 4 + width_y]
        )
        summed = summed + weight * (
            padded[:, 4 : 4 + width_x, 4 + reach : 4 + reach + width_y]
            + padded[:, 4 : 4 + width_x, 4 - reach : 4 - reach + width_y]
        )
    return summed


def inject(volume, cell_ids, values, offset):
    count_rows = volume.shape[0]
    plane_size = volume.shape[1] * volume.shape[2]
    depth_row = cell_ids // plane_size - offset
    remainder = cell_ids % plane_size
    inside = (depth_row >= 0) & (depth_row < count_rows)
    row_safe = jnp.clip(depth_row, 0, count_rows - 1)
    return volume.at[row_safe, remainder // volume.shape[2], remainder % volume.shape[2]].add(
        jnp.where(inside, values, jnp.zeros_like(values))
    )


def per_device(
    courant,
    wave_before,
    wave_current,
    adjoint_after,
    adjoint_current,
    source_cell,
    wavelet,
    receiver_cell,
    residual,
    history,
):
    slab_rows = courant.shape[0]
    first_row = lax.axis_index("depth") * slab_rows
    shot_count = lax.axis_size("shot")
    summed = jnp.zeros(courant.shape, jnp.float32)
    laplacians = []
    wave_old = wave_before[0]
    wave_now = wave_current[0]
    for moment in range(STEPS):
        extended = with_halo(wave_now, (("depth", 0),), 4)
        laplacian = laplace_core(extended)
        wave_new = 2.0 * wave_now - wave_old + courant * laplacian
        wave_new = inject(wave_new, source_cell, wavelet[0, moment : moment + 1], first_row)
        laplacians.append(laplacian)
        wave_old, wave_now = (wave_now, wave_new)
    adjoint_old = adjoint_after[0]
    adjoint_now = adjoint_current[0]
    for moment in reversed(range(STEPS)):
        extended = with_halo(courant * adjoint_now, (("depth", 0),), 4)
        adjoint_new = 2.0 * adjoint_now - adjoint_old + laplace_core(extended)
        adjoint_new = inject(adjoint_new, receiver_cell[0], residual[0, moment], first_row)
        summed = summed + adjoint_new * laplacians[moment]
        adjoint_old, adjoint_now = (adjoint_now, adjoint_new)
    grad_piece = lax.psum_scatter(summed, "shot", scatter_dimension=1, tiled=True) * (
        1.0 / (shot_count * STEPS)
    )
    displaced = history[0]
    changes = history[1]
    pair_dots = jnp.sum(displaced * changes, axis=(1, 2, 3))
    last_square = jnp.sum(changes[PAIRS - 1] * changes[PAIRS - 1])
    curvature, last_square = lax.psum((pair_dots, last_square), ("depth", "shot"))
    inverse = 1.0 / curvature
    search = grad_piece
    alphas = [None] * PAIRS
    for number in reversed(range(PAIRS)):
        alphas[number] = inverse[number] * lax.psum(
            jnp.sum(displaced[number] * search), ("depth", "shot")
        )
        search = search - alphas[number] * changes[number]
    scaled = curvature[PAIRS - 1] / last_square * search
    for number in range(PAIRS):
        correction = inverse[number] * lax.psum(
            jnp.sum(changes[number] * scaled), ("depth", "shot")
        )
        scaled = scaled + (alphas[number] - correction) * displaced[number]
    direction = -scaled
    piece_width = grad_piece.shape[1]
    own_courant = lax.dynamic_slice_in_dim(
        courant, lax.axis_index("shot") * piece_width, piece_width, 1
    )
    next_piece = own_courant + 0.05 * direction
    courant_next = lax.all_gather(next_piece, "shot", axis=1, tiled=True)
    return (grad_piece, direction, courant_next)


def solution(mesh):
    return jax.shard_map(
        per_device,
        mesh=mesh,
        in_specs=(
            P("depth", None, None),
            P("shot", "depth", None, None),
            P("shot", "depth", None, None),
            P("shot", "depth", None, None),
            P("shot", "depth", None, None),
            P("shot"),
            P("shot", None),
            P("shot", None),
            P("shot", None, None),
            P(None, None, "depth", "shot", None),
        ),
        out_specs=(P("depth", "shot", None), P("depth", "shot", None), P("depth", None, None)),
        check_vma=False,
    )
```

profile of v0, /device:TPU:1, one launch (start us, length us, event | category | flops | bytes accessed | tf_op | source)
XLA Modules:
  0.0 1048.4 jit_solution(10083528813388528675)
XLA Ops:
  7.2 1.7 slice_bitcast_fusion.1
  8.9 5.1 collective-permute-start.2
  14.1 2.9 collective-permute-start.3
  17.1 1.2 bitcast_multiply_fusion
  18.3 2.1 collective-permute-start
  20.3 5.1 collective-permute-start.1
  26.2 0.6 fusion.387
  29.4 0.8 and_reduce_fusion
  30.2 2.0 fusion.184
  32.2 24.0 %scatter_fusion = f32[16,64,128]{2,1,0:T(8,128)S(1)} fusion(f32[16,64,128]{2,1,0:T(8,128)S(1)} %fusion.184, s32[256]{0:T(256)S(1)} %bitcast.166, f32[256]{0:T(256)} %get-tuple-element.95), kind=kCustom, calls=%fused_computation | custom fusion | flops 256 | bytes 6144 | tf_op jit(solution)/shard_map/scatter-add | solution.py:61
  56.2 3.7 fusion.344
  59.9 0.7 fusion.380
  60.6 1.9 collective-permute-start.10
  62.5 5.1 collective-permute-start.11
  70.3 0.7 fusion.383
  71.1 1.9 collective-permute-start.4
  73.0 5.1 collective-permute-start.5
  78.2 8.4 fusion.59
  86.6 15.3 %scatter_fusion.1 = f32[16,64,128]{2,1,0:T(8,128)S(1)} fusion(f32[16,64,128]{2,1,0:T(8,128)S(1)} %fusion.59, s32[256]{0:T(256)S(1)} %bitcast.167, f32[256]{0:T(256)S(1)} %get-tuple-element.94), kind=kCustom, calls=%fused_computation.1 | custom fusion | flops 256 | bytes 6144 | tf_op jit(solution)/shard_map/scatter-add | solution.py:61
  101.9 3.8 multiply_add_fusion.1
  105.7 0.7 dynamic-slice.25
  108.3 0.7 fusion.379
  109.0 1.9 collective-permute-start.12
  110.9 5.1 collective-permute-start.13
  116.3 0.8 fusion.382
  117.0 1.9 collective-permute-start.6
  118.9 5.3 collective-permute-start.7
  124.3 2.2 fusion.34
  126.5 15.3 %scatter_fusion.2 = f32[16,64,128]{2,1,0:T(8,128)S(1)} fusion(f32[16,64,128]{2,1,0:T(8,128)S(1)} %fusion.34, s32[256]{0:T(256)S(1)} %bitcast.168, f32[256]{0:T(256)S(1)} %get-tuple-element.93), kind=kCustom, calls=%fused_computation.2 | custom fusion | flops 256 | bytes 6144 | tf_op jit(solution)/shard_map/scatter-add | solution.py:61
  141.8 9.8 multiply_add_fusion
  151.6 0.7 dynamic-slice.26
  154.2 0.7 fusion.378
  154.9 1.9 collective-permute-start.14
  156.9 6.2 collective-permute-start.15
  163.3 0.8 fusion.381
  164.1 1.9 collective-permute-start.8
  166.0 6.0 collective-permute-start.9
  172.1 2.2 fusion.9
  174.3 15.3 %scatter_fusion.3 = f32[16,64,128]{2,1,0:T(8,128)S(1)} fusion(f32[16,64,128]{2,1,0:T(8,128)S(1)} %fusion.9, s32[256]{0:T(256)S(1)} %bitcast.169, f32[256]{0:T(256)S(1)} %get-tuple-element.57), kind=kCustom, calls=%fused_computation.3 | custom fusion | flops 256 | bytes 6144 | tf_op jit(solution)/shard_map/scatter-add | solution.py:61
  189.6 10.4 fusion.87
  200.2 50.1 %reduce-scatter.2.cloned.1.call-done = f32[16,8,128]{2,1,0:T(8,128)} async-done(((f32[16,64,128]{2,1,0:T(8,128)}), f32[16,8,128]{2,1,0:T(8,128)}) %reduce-scatter.2.cloned.1.call-update) | async-done | bytes 65552 | tf_op jit(solution)/shard_map/reduce_scatter | solution.py:100
  250.3 1.5 fusion.362
  251.8 78.4 %all-reduce.9 = (f32[5]{0:T(128)S(1)}, f32[]{:T(128)}) all-reduce(f32[5]{0:T(128)S(1)} %multiply_reduce_fusion, f32[]{:T(128)} %get-tuple-element.55), channel_id=1, replica_groups=mesh['depth'=32,'shot'=8] {'depth','shot'}, use_global_device_ids=true, to_apply=%region_7.8 | all-reduce | flops 6 | bytes 48 | tf_op jit(solution)/shard_map/psum | solution.py:107
  330.2 0.7 fusion.386
  332.2 0.6 fusion.360
  333.4 74.3 %psum.87 = f32[]{:T(128)} all-reduce(f32[]{:T(128)} %fusion.360), channel_id=1, replica_groups=mesh['depth'=32,'shot'=8] {'depth','shot'}, use_global_device_ids=true, to_apply=%region_13.14 | all-reduce | flops 1 | bytes 8 | tf_op jit(solution)/shard_map/psum | solution.py:112
  409.0 0.6 fusion.356
  409.6 73.3 %psum.88 = f32[]{:T(128)} all-reduce(f32[]{:T(128)} %get-tuple-element.53), channel_id=1, replica_groups=mesh['depth'=32,'shot'=8] {'depth','shot'}, use_global_device_ids=true, to_apply=%region_15.16 | all-reduce | flops 1 | bytes 8 | tf_op jit(solution)/shard_map/psum | solution.py:112
  484.2 0.6 fusion.365
  484.8 74.2 %psum.89 = f32[]{:T(128)} all-reduce(f32[]{:T(128)} %get-tuple-element.40), channel_id=1, replica_groups=mesh['depth'=32,'shot'=8] {'depth','shot'}, use_global_device_ids=true, to_apply=%region_17.18 | all-reduce | flops 1 | bytes 8 | tf_op jit(solution)/shard_map/psum | solution.py:112
  560.9 73.5 %all-reduce.8 = (f32[]{:T(128)}, f32[]{:T(128)}) all-reduce(f32[]{:T(128)} %get-tuple-element.51, f32[]{:T(128)} %get-tuple-element.39), channel_id=1, replica_groups=mesh['depth'=32,'shot'=8] {'depth','shot'}, use_global_device_ids=true, to_apply=%region_19.20 | all-reduce | flops 2 | bytes 16 | tf_op jit(solution)/shard_map/psum | solution.py:112
  636.9 0.6 fusion.347
  637.6 74.2 %psum.91 = f32[]{:T(128)} all-reduce(f32[]{:T(128)} %fusion.347), channel_id=1, replica_groups=mesh['depth'=32,'shot'=8] {'depth','shot'}, use_global_device_ids=true, to_apply=%region_21.22 | all-reduce | flops 1 | bytes 8 | tf_op jit(solution)/shard_map/psum | solution.py:118
  713.1 0.6 fusion.351
  713.7 73.4 %psum.92 = f32[]{:T(128)} all-reduce(f32[]{:T(128)} %get-tuple-element.49), channel_id=1, replica_groups=mesh['depth'=32,'shot'=8] {'depth','shot'}, use_global_device_ids=true, to_apply=%region_23.24 | all-reduce | flops 1 | bytes 8 | tf_op jit(solution)/shard_map/psum | solution.py:118
  788.4 0.6 fusion.355
  789.0 74.2 %psum.93 = f32[]{:T(128)} all-reduce(f32[]{:T(128)} %fusion.355), channel_id=1, replica_groups=mesh['depth'=32,'shot'=8] {'depth','shot'}, use_global_device_ids=true, to_apply=%region_25.26 | all-reduce | flops 1 | bytes 8 | tf_op jit(solution)/shard_map/psum | solution.py:118
  864.4 0.6 fusion.359
  865.0 73.4 %psum.94 = f32[]{:T(128)} all-reduce(f32[]{:T(128)} %get-tuple-element.47), channel_id=1, replica_groups=mesh['depth'=32,'shot'=8] {'depth','shot'}, use_global_device_ids=true, to_apply=%region_27.28 | all-reduce | flops 1 | bytes 8 | tf_op jit(solution)/shard_map/psum | solution.py:118
  939.8 0.6 fusion.367
  940.4 74.1 %psum.95 = f32[]{:T(128)} all-reduce(f32[]{:T(128)} %fusion.367), channel_id=1, replica_groups=mesh['depth'=32,'shot'=8] {'depth','shot'}, use_global_device_ids=true, to_apply=%region_29.30 | all-reduce | flops 1 | bytes 8 | tf_op jit(solution)/shard_map/psum | solution.py:118
  1015.8 0.7 multiply_add_fusion.2
  1016.4 24.3 %all_gather.3 = f32[16,64,128]{2,1,0:T(8,128)S(1)} all-gather(f32[16,8,128]{2,1,0:T(8,128)S(1)} %get-tuple-element.45), channel_id=1, replica_groups=mesh['depth'=32,'shot'=8] {'shot'}, dimensions={1}, use_global_device_ids=true | all-gather | bytes 589824 | tf_op jit(solution)/shard_map/all_gather | solution.py:128
  1040.7 0.8 copy.22
  (65 shorter events, 3.2 us)
Async XLA Ops:
  7.2 9.9 copy-start
  7.2 243.2 %reduce-scatter.2.cloned.1.call-start = ((), (), s32[]{:S(2)}) async-start(), calls=%async_computation.1 | async-start | bytes 589824 | tf_op jit(solution)/shard_map/reduce_scatter | solution.py:100
  8.9 47.3 %collective-permute-start.2 = (f32[4,64,128]{2,1,0:T(8,128)}, f32[4,64,128]{2,1,0:T(8,128)S(1)}, u32[]{:S(2)}, u32[]{:S(2)}) collective-permute-start(f32[4,64,128]{2,1,0:T(8,128)} %get-tuple-element.80), channel_id=1, source_target_pairs={{8,0},{16,8},{24,16},{32,24},{40,32},{48,40},{56,48},{64,56},{72,6... | collective-permute-start | bytes 393224 | tf_op jit(solution)/shard_map/ppermute | solution.py:23
  14.1 11.4 %copy-start.14 = (f32[1,4,256]{2,1,0:T(4,128)S(1)}, f32[1,4,256]{2,1,0:T(4,128)}, u32[]{:S(2)}) copy-start(f32[1,4,256]{2,1,0:T(4,128)} %param.24) | copy-start | bytes 12292
  14.1 11.5 %copy-start.15 = (s32[1,256]{1,0:T(1,128)S(1)}, s32[1,256]{1,0:T(1,128)}, u32[]{:S(2)}) copy-start(s32[1,256]{1,0:T(1,128)} %param.23) | copy-start | bytes 3076
  14.1 12.1 %copy-start.13 = (f32[1,4]{1,0:T(1,128)S(1)}, f32[1,4]{1,0:T(1,128)}, u32[]{:S(2)}) copy-start(f32[1,4]{1,0:T(1,128)} %param.22) | copy-start | bytes 52
  14.1 42.1 %collective-permute-start.3 = (f32[4,64,128]{2,1,0:T(8,128)S(1)}, f32[4,64,128]{2,1,0:T(8,128)S(1)}, u32[]{:S(2)}, u32[]{:S(2)}) collective-permute-start(f32[4,64,128]{2,1,0:T(8,128)S(1)} %get-tuple-element.81), channel_id=1, source_target_pairs={{0,8},{8,16},{16,24},{24,32},{32,40},{40,48},{48,56},{56,64},{64,7... | collective-permute-start | bytes 393224 | tf_op jit(solution)/shard_map/ppermute | solution.py:21
  17.1 13.2 %copy-start.12 = (f32[1,16,64,128]{3,2,1,0:T(8,128)S(1)}, f32[1,16,64,128]{3,2,1,0:T(8,128)}, u32[]{:S(2)}) copy-start(f32[1,16,64,128]{3,2,1,0:T(8,128)} %param.19) | copy-start | bytes 1572868
  18.2 11.2 %copy-start.16 = (s32[3]{0:T(128)S(1)}, s32[3]{0:T(128)}, u32[]{:S(2)}) copy-start(s32[3]{0:T(128)} %constant.251.clone.1) | copy-start | bytes 40
  18.2 12.0 %copy-start.3 = (f32[1,16,64,128]{3,2,1,0:T(8,128)S(1)}, f32[1,16,64,128]{3,2,1,0:T(8,128)}, u32[]{:S(2)}) copy-start(f32[1,16,64,128]{3,2,1,0:T(8,128)} %param.20) | copy-start | bytes 1572868
  18.3 11.9 %collective-permute-start = (f32[4,64,128]{2,1,0:T(8,128)S(1)}, f32[4,64,128]{2,1,0:T(8,128)S(1)}, u32[]{:S(2)}, u32[]{:S(2)}) collective-permute-start(f32[4,64,128]{2,1,0:T(8,128)S(1)} %get-tuple-element.82), channel_id=1, source_target_pairs={{8,0},{16,8},{24,16},{32,24},{40,32},{48,40},{56,48},{64,56},{72,6... | collective-permute-start | bytes 393224 | tf_op jit(solution)/shard_map/ppermute | solution.py:23
  20.3 9.9 collective-permute-start.1
  32.2 24.0 %copy-start.2 = (f32[1,16,64,128]{3,2,1,0:T(8,128)S(1)}, f32[1,16,64,128]{3,2,1,0:T(8,128)}, u32[]{:S(2)}) copy-start(f32[1,16,64,128]{3,2,1,0:T(8,128)} %param.18) | copy-start | bytes 1572868
  59.9 18.3 %copy-start.8 = (f32[16,64,128]{2,1,0:T(8,128)}, f32[16,64,128]{2,1,0:T(8,128)S(1)}, u32[]{:S(2)}) copy-start(f32[16,64,128]{2,1,0:T(8,128)S(1)} %get-tuple-element.73) | copy-start | bytes 1572868
  60.6 17.6 %collective-permute-start.10 = (f32[4,64,128]{2,1,0:T(8,128)}, f32[4,64,128]{2,1,0:T(8,128)S(1)}, u32[]{:S(2)}, u32[]{:S(2)}) collective-permute-start(f32[4,64,128]{2,1,0:T(8,128)} %get-tuple-element.71), channel_id=1, source_target_pairs={{8,0},{16,8},{24,16},{32,24},{40,32},{48,40},{56,48},{64,56},{72,6... | collective-permute-start | bytes 393224 | tf_op jit(solution)/shard_map/ppermute | solution.py:23
  62.5 15.7 %collective-permute-start.11 = (f32[4,64,128]{2,1,0:T(8,128)S(1)}, f32[4,64,128]{2,1,0:T(8,128)S(1)}, u32[]{:S(2)}, u32[]{:S(2)}) collective-permute-start(f32[4,64,128]{2,1,0:T(8,128)S(1)} %get-tuple-element.72), channel_id=1, source_target_pairs={{0,8},{8,16},{16,24},{24,32},{32,40},{40,48},{48,56},{56,64},{64,7... | collective-permute-start | bytes 393224 | tf_op jit(solution)/shard_map/ppermute | solution.py:21
  71.1 30.8 %collective-permute-start.4 = (f32[4,64,128]{2,1,0:T(8,128)}, f32[4,64,128]{2,1,0:T(8,128)}, u32[]{:S(2)}, u32[]{:S(2)}) collective-permute-start(f32[4,64,128]{2,1,0:T(8,128)} %get-tuple-element.78), channel_id=1, source_target_pairs={{8,0},{16,8},{24,16},{32,24},{40,32},{48,40},{56,48},{64,56},{72,6... | collective-permute-start | bytes 393224 | tf_op jit(solution)/shard_map/ppermute | solution.py:23
  73.0 28.9 %collective-permute-start.5 = (f32[4,64,128]{2,1,0:T(8,128)}, f32[4,64,128]{2,1,0:T(8,128)}, u32[]{:S(2)}, u32[]{:S(2)}) collective-permute-start(f32[4,64,128]{2,1,0:T(8,128)} %get-tuple-element.79), channel_id=1, source_target_pairs={{0,8},{8,16},{16,24},{24,32},{32,40},{40,48},{48,56},{56,64},{64,7... | collective-permute-start | bytes 393224 | tf_op jit(solution)/shard_map/ppermute | solution.py:21
  105.7 5.3 copy-start.9
  109.0 15.2 %collective-permute-start.12 = (f32[4,64,128]{2,1,0:T(8,128)}, f32[4,64,128]{2,1,0:T(8,128)S(1)}, u32[]{:S(2)}, u32[]{:S(2)}) collective-permute-start(f32[4,64,128]{2,1,0:T(8,128)} %get-tuple-element.68), channel_id=1, source_target_pairs={{8,0},{16,8},{24,16},{32,24},{40,32},{48,40},{56,48},{64,56},{72,6... | collective-permute-start | bytes 393224 | tf_op jit(solution)/shard_map/ppermute | solution.py:23
  110.9 13.3 %collective-permute-start.13 = (f32[4,64,128]{2,1,0:T(8,128)}, f32[4,64,128]{2,1,0:T(8,128)}, u32[]{:S(2)}, u32[]{:S(2)}) collective-permute-start(f32[4,64,128]{2,1,0:T(8,128)} %get-tuple-element.69), channel_id=1, source_target_pairs={{0,8},{8,16},{16,24},{24,32},{32,40},{40,48},{48,56},{56,64},{64,7... | collective-permute-start | bytes 393224 | tf_op jit(solution)/shard_map/ppermute | solution.py:21
  116.1 8.2 copy-start.10
  116.2 8.0 copy-start.5
  117.0 24.8 %collective-permute-start.6 = (f32[4,64,128]{2,1,0:T(8,128)}, f32[4,64,128]{2,1,0:T(8,128)S(1)}, u32[]{:S(2)}, u32[]{:S(2)}) collective-permute-start(f32[4,64,128]{2,1,0:T(8,128)} %get-tuple-element.76), channel_id=1, source_target_pairs={{8,0},{16,8},{24,16},{32,24},{40,32},{48,40},{56,48},{64,56},{72,6... | collective-permute-start | bytes 393224 | tf_op jit(solution)/shard_map/ppermute | solution.py:23
  118.9 22.9 %collective-permute-start.7 = (f32[4,64,128]{2,1,0:T(8,128)}, f32[4,64,128]{2,1,0:T(8,128)S(1)}, u32[]{:S(2)}, u32[]{:S(2)}) collective-permute-start(f32[4,64,128]{2,1,0:T(8,128)} %get-tuple-element.77), channel_id=1, source_target_pairs={{0,8},{8,16},{16,24},{24,32},{32,40},{40,48},{48,56},{56,64},{64,7... | collective-permute-start | bytes 393224 | tf_op jit(solution)/shard_map/ppermute | solution.py:21
  151.6 5.2 copy-start.6
  154.9 17.1 %collective-permute-start.14 = (f32[4,64,128]{2,1,0:T(8,128)}, f32[4,64,128]{2,1,0:T(8,128)S(1)}, u32[]{:S(2)}, u32[]{:S(2)}) collective-permute-start(f32[4,64,128]{2,1,0:T(8,128)} %get-tuple-element.65), channel_id=1, source_target_pairs={{8,0},{16,8},{24,16},{32,24},{40,32},{48,40},{56,48},{64,56},{72,6... | collective-permute-start | bytes 393224 | tf_op jit(solution)/shard_map/ppermute | solution.py:23
  156.9 15.2 %collective-permute-start.15 = (f32[4,64,128]{2,1,0:T(8,128)}, f32[4,64,128]{2,1,0:T(8,128)}, u32[]{:S(2)}, u32[]{:S(2)}) collective-permute-start(f32[4,64,128]{2,1,0:T(8,128)} %get-tuple-element.66), channel_id=1, source_target_pairs={{0,8},{8,16},{16,24},{24,32},{32,40},{40,48},{48,56},{56,64},{64,7... | collective-permute-start | bytes 393224 | tf_op jit(solution)/shard_map/ppermute | solution.py:21
  163.1 9.0 copy-start.7
  163.3 8.8 copy-start.4
  164.1 25.5 %collective-permute-start.8 = (f32[4,64,128]{2,1,0:T(8,128)}, f32[4,64,128]{2,1,0:T(8,128)S(1)}, u32[]{:S(2)}, u32[]{:S(2)}) collective-permute-start(f32[4,64,128]{2,1,0:T(8,128)} %get-tuple-element.74), channel_id=1, source_target_pairs={{8,0},{16,8},{24,16},{32,24},{40,32},{48,40},{56,48},{64,56},{72,6... | collective-permute-start | bytes 393224 | tf_op jit(solution)/shard_map/ppermute | solution.py:23
  166.0 23.6 %collective-permute-start.9 = (f32[4,64,128]{2,1,0:T(8,128)}, f32[4,64,128]{2,1,0:T(8,128)S(1)}, u32[]{:S(2)}, u32[]{:S(2)}) collective-permute-start(f32[4,64,128]{2,1,0:T(8,128)} %get-tuple-element.75), channel_id=1, source_target_pairs={{0,8},{8,16},{16,24},{24,32},{32,40},{40,48},{48,56},{56,64},{64,7... | collective-permute-start | bytes 393224 | tf_op jit(solution)/shard_map/ppermute | solution.py:21
  189.6 10.5 copy-start.1
  251.8 385.8 %copy-start.11 = (f32[16,8,128]{2,1,0:T(8,128)}, f32[16,8,128]{2,1,0:T(8,128)S(1)}, u32[]{:S(2)}) copy-start(f32[16,8,128]{2,1,0:T(8,128)S(1)} %get-tuple-element.102) | copy-start | bytes 196612
Sparse Core Ops, SparseCore 0:
  200.2 50.1 reduce-scatter.1
where the time goes:
time: 1060 us; the launch traced here: 1050 us
  blocking collectives  767 us (72%)
  other arithmetic  123 us (12%)
  starting transfers between devices  59.8 us (6%)
  waiting for transfers between devices  50.2 us (5%)
  between operations  37.1 us (4%)
  local copies, waits for them, and re-layouts  11.3 us (1%)
    psum x5, blocking collectives, per_device(): lax.psum(jnp.sum(changes[number] * scaled), ('depth', 'shot'))  369 us
    psum x4, blocking collectives, per_device(): lax.psum(jnp.sum(displaced[number] * search), ('depth', 'shot'))  295 us
    psum x1, blocking collectives, per_device(): lax.psum((pair_dots, last_square), ('depth', 'shot'))  78.4 us
    scatter-add x4, other arithmetic, inject(): volume.at[row_safe, remainder // volume.shape[2], remainder % volume.shap...  69.7 us
    reduce_scatter x1, waiting for transfers between devices, per_device(): lax.psum_scatter(summed, 'shot', scatter_dimension=1, tiled=True)  50.1 us
    ppermute x8, starting transfers between devices, with_halo(): lax.ppermute(tail, axis, [(i, (i + 1) % count) for i in range(ends)])  41.1 us
    all_gather x1, blocking collectives, per_device(): courant_next = lax.all_gather(next_piece, 'shot', axis=1, tiled=True)  24.3 us
  transfers between devices with their start and end apart: 17, of which 1 were waited for; matrix products, arithmetic and copies ran while one was open for 9% of the time, Pallas kernels for 0%

commit v1 on v0

--- a/solution.py
+++ b/solution.py
@@ -102,23 +102,41 @@
     )
     displaced = history[0]
     changes = history[1]
-    pair_dots = jnp.sum(displaced * changes, axis=(1, 2, 3))
-    last_square = jnp.sum(changes[PAIRS - 1] * changes[PAIRS - 1])
-    curvature, last_square = lax.psum((pair_dots, last_square), ("depth", "shot"))
-    inverse = 1.0 / curvature
-    search = grad_piece
+    step_change = jnp.einsum("izxy,jzxy->ij", displaced, changes, precision=lax.Precision.HIGHEST)
+    change_change = jnp.einsum("izxy,jzxy->ij", changes, changes, precision=lax.Precision.HIGHEST)
+    step_grad = jnp.sum(displaced * grad_piece, axis=(1, 2, 3))
+    change_grad = jnp.sum(changes * grad_piece, axis=(1, 2, 3))
+    packed = jnp.concatenate(
+        [step_change, change_change, step_grad[None], change_grad[None]], axis=0
+    )
+    packed = lax.psum(packed, ("depth", "shot"))
+    step_change = packed[:PAIRS]
+    change_change = packed[PAIRS : 2 * PAIRS]
+    step_grad = packed[2 * PAIRS]
+    change_grad = packed[2 * PAIRS + 1]
+    inverse = [1.0 / step_change[i, i] for i in range(PAIRS)]
     alphas = [None] * PAIRS
-    for number in reversed(range(PAIRS)):
-        alphas[number] = inverse[number] * lax.psum(
-            jnp.sum(displaced[number] * search), ("depth", "shot")
-        )
-        search = search - alphas[number] * changes[number]
-    scaled = curvature[PAIRS - 1] / last_square * search
-    for number in range(PAIRS):
-        correction = inverse[number] * lax.psum(
-            jnp.sum(changes[number] * scaled), ("depth", "shot")
-        )
-        scaled = scaled + (alphas[number] - correction) * displaced[number]
+    for i in reversed(range(PAIRS)):
+        value = step_grad[i]
+        for j in range(i + 1, PAIRS):
+            value = value - alphas[j] * step_change[i, j]
+        alphas[i] = inverse[i] * value
+    gamma = step_change[PAIRS - 1, PAIRS - 1] / change_change[PAIRS - 1, PAIRS - 1]
+    gains = []
+    for i in range(PAIRS):
+        value = change_grad[i]
+        for j in range(PAIRS):
+            value = value - alphas[j] * change_change[i, j]
+        value = gamma * value
+        for j in range(i):
+            value = value + gains[j] * step_change[j, i]
+        gains.append(alphas[i] - inverse[i] * value)
+    scaled = grad_piece
+    for i in range(PAIRS):
+        scaled = scaled - alphas[i] * changes[i]
+    scaled = gamma * scaled
+    for i in range(PAIRS):
+        scaled = scaled + gains[i] * displaced[i]
     direction = -scaled
     piece_width = grad_piece.shape[1]
     own_courant = lax.dynamic_slice_in_dim(

time: 1060 us -> 400 us (0.38)
  blocking collectives: 767 us -> 103 us
  between operations: 37.1 us -> 61.9 us
  other arithmetic: 123 us -> 111 us
    psum x10 -> x1, blocking collectives: 743 us -> 78.4 us  [per_device(): packed = lax.psum(packed, ('depth', 'shot'))]
  transfers between devices with their start and end apart: 17 -> 17, of which waited for: 1 -> 1; matrix products, arithmetic and copies ran while one was open for 9% -> 24% of each run, Pallas kernels for 0% -> 0%
where the time goes in v1:
time: 400 us; the launch traced here: 394 us
  other arithmetic  111 us (28%)
  blocking collectives  103 us (26%)
  between operations  61.9 us (15%)
  starting transfers between devices  59.7 us (15%)
  waiting for transfers between devices  46.7 us (12%)
  local copies, waits for them, and re-layouts  9.48 us (2%)
    psum x1, blocking collectives, per_device(): packed = lax.psum(packed, ('depth', 'shot'))  78.4 us
    scatter-add x4, other arithmetic, inject(): volume.at[row_safe, remainder // volume.shape[2], remainder % volume.shap...  69.7 us
    reduce_scatter x1, waiting for transfers between devices, per_device(): lax.psum_scatter(summed, 'shot', scatter_dimension=1, tiled=True)  46.6 us
    ppermute x8, starting transfers between devices, with_halo(): lax.ppermute(tail, axis, [(i, (i + 1) % count) for i in range(ends)])  40.9 us
    all_gather x1, blocking collectives, per_device(): courant_next = lax.all_gather(next_piece, 'shot', axis=1, tiled=True)  24.9 us
    ppermute x8, starting transfers between devices, with_halo(): lax.ppermute(head, axis, [((i + 1) % count, i) for i in range(ends)])  18.7 us
    add x3, other arithmetic, per_device(): wave_new = 2.0 * wave_now - wave_old + courant * laplacian  17 us
    add x4, other arithmetic, per_device(): adjoint_new = 2.0 * adjoint_now - adjoint_old + laplace_core(extended)  15.3 us
  transfers between devices with their start and end apart: 17, of which 1 were waited for; matrix products, arithmetic and copies ran while one was open for 24% of the time, Pallas kernels for 0%

profile of v1, /device:TPU:1, one launch (start us, length us, event | category | flops | bytes accessed | tf_op | source)
XLA Modules:
  0.0 394.4 jit_solution(11437620847095359479)
XLA Ops:
  7.2 0.0 reduce-scatter.2.cloned.1.call-start
  7.2 1.3 bitcast_multiply_fusion
  8.5 0.0 copy-start.1
  8.6 0.0 copy-start.14
  8.6 0.0 copy-start.15
  8.6 0.0 copy-start.13
  8.6 0.0 copy-start.16
  8.6 5.3 %collective-permute-start = (f32[4,64,128]{2,1,0:T(8,128)S(1)}, f32[4,64,128]{2,1,0:T(8,128)S(1)}, u32[]{:S(2)}, u32[]{:S(2)}) collective-permute-start(f32[4,64,128]{2,1,0:T(8,128)S(1)} %get-tuple-element.70), channel_id=1, source_target_pairs={{8,0},{16,8},{24,16},{32,24},{40,32},{48,40},{56,48},{64,56},{72,6... | collective-permute-start | bytes 393224 | tf_op jit(solution)/shard_map/ppermute | solution.py:23
  13.9 2.8 collective-permute-start.1
  16.8 1.9 collective-permute-start.2
  18.7 5.1 %collective-permute-start.3 = (f32[4,64,128]{2,1,0:T(8,128)S(1)}, f32[4,64,128]{2,1,0:T(8,128)S(1)}, u32[]{:S(2)}, u32[]{:S(2)}) collective-permute-start(f32[4,64,128]{2,1,0:T(8,128)S(1)} %get-tuple-element.69), channel_id=1, source_target_pairs={{0,8},{8,16},{16,24},{24,32},{32,40},{40,48},{48,56},{56,64},{64,7... | collective-permute-start | bytes 393224 | tf_op jit(solution)/shard_map/ppermute | solution.py:21
  24.0 0.6 broadcast_select_fusion.1
  24.5 0.7 fusion.369
  27.9 0.7 and_reduce_fusion
  28.7 1.9 fusion.184
  30.6 24.0 %scatter_fusion = f32[16,64,128]{2,1,0:T(8,128)S(1)} fusion(f32[16,64,128]{2,1,0:T(8,128)S(1)} %fusion.184, s32[256]{0:T(256)S(1)} %bitcast.180, f32[256]{0:T(256)} %get-tuple-element.128), kind=kCustom, calls=%fused_computation | custom fusion | flops 256 | bytes 6144 | tf_op jit(solution)/shard_map/scatter-add | solution.py:61
  54.6 3.7 fusion.348
  58.3 0.7 dynamic-slice.24
  60.9 0.1 scatter-add.44
  61.1 1.9 collective-permute-start.10
  63.0 5.1 %collective-permute-start.11 = (f32[4,64,128]{2,1,0:T(8,128)S(1)}, f32[4,64,128]{2,1,0:T(8,128)S(1)}, u32[]{:S(2)}, u32[]{:S(2)}) collective-permute-start(f32[4,64,128]{2,1,0:T(8,128)S(1)} %get-tuple-element.60), channel_id=1, source_target_pairs={{0,8},{8,16},{16,24},{24,32},{32,40},{40,48},{48,56},{56,64},{64,7... | collective-permute-start | bytes 393224 | tf_op jit(solution)/shard_map/ppermute | solution.py:21
  68.2 0.7 fusion.363
  68.8 1.9 collective-permute-start.4
  70.7 5.1 %collective-permute-start.5 = (f32[4,64,128]{2,1,0:T(8,128)S(1)}, f32[4,64,128]{2,1,0:T(8,128)S(1)}, u32[]{:S(2)}, u32[]{:S(2)}) collective-permute-start(f32[4,64,128]{2,1,0:T(8,128)S(1)} %get-tuple-element.67), channel_id=1, source_target_pairs={{0,8},{8,16},{16,24},{24,32},{32,40},{40,48},{48,56},{56,64},{64,7... | collective-permute-start | bytes 393224 | tf_op jit(solution)/shard_map/ppermute | solution.py:21
  75.9 9.1 %fusion.59 = f32[16,64,128]{2,1,0:T(8,128)S(1)} fusion(f32[16,64,128]{2,1,0:T(8,128)} %copy-done.6, f32[4,64,128]{2,1,0:T(8,128)S(1)} %collective-permute-done.11, f32[4,64,128]{2,1,0:T(8,128)S(1)} %collective-permute-done.10, f32[1,16,64,128]{3,2,1,0:T(8,128)S(1)} %copy-done.2, f32[16,64,128]{2,1,0:T(8,128)S(1)} %scatter_fusion), kind=kLoop, calls=%fused_computation.289 | loop fusion | flops 6291456 | bytes 2359296 | tf_op jit(solution)/shard_map/add | solution.py:96
  85.1 15.2 %scatter_fusion.1 = f32[16,64,128]{2,1,0:T(8,128)S(1)} fusion(f32[16,64,128]{2,1,0:T(8,128)S(1)} %fusion.59, s32[256]{0:T(256)S(1)} %bitcast.181, f32[256]{0:T(256)S(1)} %get-tuple-element.127), kind=kCustom, calls=%fused_computation.1 | custom fusion | flops 256 | bytes 6144 | tf_op jit(solution)/shard_map/scatter-add | solution.py:61
  100.3 2.7 multiply_add_fusion.1
  103.1 1.9 collective-permute-start.12
  105.0 5.1 %collective-permute-start.13 = (f32[4,64,128]{2,1,0:T(8,128)S(1)}, f32[4,64,128]{2,1,0:T(8,128)S(1)}, u32[]{:S(2)}, u32[]{:S(2)}) collective-permute-start(f32[4,64,128]{2,1,0:T(8,128)S(1)} %get-tuple-element.57), channel_id=1, source_target_pairs={{0,8},{8,16},{16,24},{24,32},{32,40},{40,48},{48,56},{56,64},{64,7... | collective-permute-start | bytes 393224 | tf_op jit(solution)/shard_map/ppermute | solution.py:21
  110.2 0.6 dynamic-slice.25
  112.7 0.1 scatter-add.45
  112.9 0.7 fusion.362
  113.6 1.9 collective-permute-start.6
  115.5 5.3 %collective-permute-start.7 = (f32[4,64,128]{2,1,0:T(8,128)}, f32[4,64,128]{2,1,0:T(8,128)}, u32[]{:S(2)}, u32[]{:S(2)}) collective-permute-start(f32[4,64,128]{2,1,0:T(8,128)} %get-tuple-element.65), channel_id=1, source_target_pairs={{0,8},{8,16},{16,24},{24,32},{32,40},{40,48},{48,56},{56,64},{64,7... | collective-permute-start | bytes 393224 | tf_op jit(solution)/shard_map/ppermute | solution.py:21
  120.8 2.0 fusion.34
  122.8 15.2 %scatter_fusion.2 = f32[16,64,128]{2,1,0:T(8,128)S(1)} fusion(f32[16,64,128]{2,1,0:T(8,128)S(1)} %fusion.34, s32[256]{0:T(256)S(1)} %bitcast.182, f32[256]{0:T(256)S(1)} %get-tuple-element.126), kind=kCustom, calls=%fused_computation.2 | custom fusion | flops 256 | bytes 6144 | tf_op jit(solution)/shard_map/scatter-add | solution.py:61
  138.1 10.6 %multiply_add_fusion = (f32[16,64,128]{2,1,0:T(8,128)S(1)}, f32[16,64,128]{2,1,0:T(8,128)}, f32[16,64,128]{2,1,0:T(8,128)S(1)}) fusion(f32[16,64,128]{2,1,0:T(8,128)S(1)} %copy-done, f32[16,64,128]{2,1,0:T(8,128)S(1)} %scatter-add.44, f32[16,64,128]{2,1,0:T(8,128)} %copy-done.3, f32[4,64,128]{2,1,0:T(8,128)} %collective-permute-done.7, ...), kind=kLoop, calls=%fused_computation.602 | loop fusion | flops 6553600 | bytes 3932160 | tf_op jit(solution)/shard_map/add | solution.py:88
  148.7 1.9 collective-permute-start.14
  150.6 6.2 %collective-permute-start.15 = (f32[4,64,128]{2,1,0:T(8,128)S(1)}, f32[4,64,128]{2,1,0:T(8,128)}, u32[]{:S(2)}, u32[]{:S(2)}) collective-permute-start(f32[4,64,128]{2,1,0:T(8,128)S(1)} %get-tuple-element.54), channel_id=1, source_target_pairs={{0,8},{8,16},{16,24},{24,32},{32,40},{40,48},{48,56},{56,64},{64,7... | collective-permute-start | bytes 393224 | tf_op jit(solution)/shard_map/ppermute | solution.py:21
  156.9 0.6 dynamic-slice.26
  159.4 0.1 scatter-add.46
  159.5 0.7 fusion.361
  160.3 1.9 collective-permute-start.8
  162.2 6.0 %collective-permute-start.9 = (f32[4,64,128]{2,1,0:T(8,128)}, f32[4,64,128]{2,1,0:T(8,128)S(1)}, u32[]{:S(2)}, u32[]{:S(2)}) collective-permute-start(f32[4,64,128]{2,1,0:T(8,128)} %get-tuple-element.63), channel_id=1, source_target_pairs={{0,8},{8,16},{16,24},{24,32},{32,40},{40,48},{48,56},{56,64},{64,7... | collective-permute-start | bytes 393224 | tf_op jit(solution)/shard_map/ppermute | solution.py:21
  168.2 2.2 fusion.9
  170.5 15.2 %scatter_fusion.3 = f32[16,64,128]{2,1,0:T(8,128)S(1)} fusion(f32[16,64,128]{2,1,0:T(8,128)S(1)} %fusion.9, s32[256]{0:T(256)S(1)} %bitcast.183, f32[256]{0:T(256)S(1)} %get-tuple-element.43), kind=kCustom, calls=%fused_computation.3 | custom fusion | flops 256 | bytes 6144 | tf_op jit(solution)/shard_map/scatter-add | solution.py:61
  185.8 3.9 fusion.87
  189.7 0.0 reduce-scatter.2.cloned.1.call-update
  189.7 1.1 fusion.357
  190.8 1.2 convolution_bitcast_fusion
  192.1 1.4 convolution_bitcast_fusion.1
  193.4 46.6 %reduce-scatter.2.cloned.1.call-done = f32[16,8,128]{2,1,0:T(8,128)} async-done(((f32[16,64,128]{2,1,0:T(8,128)}), f32[16,8,128]{2,1,0:T(8,128)}) %reduce-scatter.2.cloned.1.call-update) | async-done | bytes 65552 | tf_op jit(solution)/shard_map/reduce_scatter | solution.py:100
  240.1 0.8 broadcast_multiply_fusion
  240.9 0.5 fusion.347
  241.5 0.1 copy.21
  241.6 0.1 copy.22
  241.7 0.1 pad_maximum_fusion.16
  241.7 78.4 %psum.7 = f32[12,5]{0,1:T(8,128)S(1)} all-reduce(f32[12,5]{0,1:T(8,128)S(1)} %pad_maximum_fusion.16), channel_id=1, replica_groups=mesh['depth'=32,'shot'=8] {'depth','shot'}, use_global_device_ids=true, to_apply=%region_8.9 | all-reduce | flops 60 | bytes 480 | tf_op jit(solution)/shard_map/psum | solution.py:112
  320.1 0.7 fusion.366
  320.8 0.7 fusion.367
  321.5 0.7 fusion.365
  361.1 0.7 multiply_add_fusion.2
  361.8 24.9 %all_gather.3 = f32[16,64,128]{2,1,0:T(8,128)S(1)} all-gather(f32[16,8,128]{2,1,0:T(8,128)S(1)} %get-tuple-element.41), channel_id=1, replica_groups=mesh['depth'=32,'shot'=8] {'shot'}, dimensions={1}, use_global_device_ids=true | all-gather | bytes 589824 | tf_op jit(solution)/shard_map/all_gather | solution.py:146
  386.7 0.8 copy.49
  (54 shorter events, 0.3 us)
Async XLA Ops:
  7.2 232.9 %reduce-scatter.2.cloned.1.call-start = ((), (), s32[]{:S(2)}) async-start(), calls=%async_computation.1 | async-start | bytes 589824 | tf_op jit(solution)/shard_map/reduce_scatter | solution.py:100
  7.2 21.4 %copy-start.10 = (f32[1,16,64,128]{3,2,1,0:T(8,128)S(1)}, f32[1,16,64,128]{3,2,1,0:T(8,128)}, u32[]{:S(2)}) copy-start(f32[1,16,64,128]{3,2,1,0:T(8,128)} %param.19) | copy-start | bytes 1572868
  8.5 8.2 %copy-start.1 = (f32[1,16,64,128]{3,2,1,0:T(8,128)S(1)}, f32[1,16,64,128]{3,2,1,0:T(8,128)}, u32[]{:S(2)}) copy-start(f32[1,16,64,128]{3,2,1,0:T(8,128)} %param.18) | copy-start | bytes 1572868
  8.6 15.3 %copy-start.14 = (f32[1,4,256]{2,1,0:T(4,128)S(1)}, f32[1,4,256]{2,1,0:T(4,128)}, u32[]{:S(2)}) copy-start(f32[1,4,256]{2,1,0:T(4,128)} %param.24) | copy-start | bytes 12292
  8.6 15.3 %copy-start.15 = (s32[1,256]{1,0:T(1,128)S(1)}, s32[1,256]{1,0:T(1,128)}, u32[]{:S(2)}) copy-start(s32[1,256]{1,0:T(1,128)} %param.23) | copy-start | bytes 3076
  8.6 16.0 %copy-start.13 = (f32[1,4]{1,0:T(1,128)S(1)}, f32[1,4]{1,0:T(1,128)}, u32[]{:S(2)}) copy-start(f32[1,4]{1,0:T(1,128)} %param.22) | copy-start | bytes 52
  8.6 19.3 %copy-start.16 = (s32[3]{0:T(128)S(1)}, s32[3]{0:T(128)}, u32[]{:S(2)}) copy-start(s32[3]{0:T(128)} %constant.255.clone.1) | copy-start | bytes 40
  8.6 20.0 %copy-start.2 = (f32[1,16,64,128]{3,2,1,0:T(8,128)S(1)}, f32[1,16,64,128]{3,2,1,0:T(8,128)}, u32[]{:S(2)}) copy-start(f32[1,16,64,128]{3,2,1,0:T(8,128)} %param.20) | copy-start | bytes 1572868
  8.6 20.0 %collective-permute-start = (f32[4,64,128]{2,1,0:T(8,128)S(1)}, f32[4,64,128]{2,1,0:T(8,128)S(1)}, u32[]{:S(2)}, u32[]{:S(2)}) collective-permute-start(f32[4,64,128]{2,1,0:T(8,128)S(1)} %get-tuple-element.70), channel_id=1, source_target_pairs={{8,0},{16,8},{24,16},{32,24},{40,32},{48,40},{56,48},{64,56},{72,6... | collective-permute-start | bytes 393224 | tf_op jit(solution)/shard_map/ppermute | solution.py:23
  13.9 14.7 %collective-permute-start.1 = (f32[4,64,128]{2,1,0:T(8,128)S(1)}, f32[4,64,128]{2,1,0:T(8,128)S(1)}, u32[]{:S(2)}, u32[]{:S(2)}) collective-permute-start(f32[4,64,128]{2,1,0:T(8,128)S(1)} %get-tuple-element.71), channel_id=1, source_target_pairs={{0,8},{8,16},{16,24},{24,32},{32,40},{40,48},{48,56},{56,64},{64,7... | collective-permute-start | bytes 393224 | tf_op jit(solution)/shard_map/ppermute | solution.py:21
  16.8 37.8 %collective-permute-start.2 = (f32[4,64,128]{2,1,0:T(8,128)S(1)}, f32[4,64,128]{2,1,0:T(8,128)S(1)}, u32[]{:S(2)}, u32[]{:S(2)}) collective-permute-start(f32[4,64,128]{2,1,0:T(8,128)S(1)} %get-tuple-element.68), channel_id=1, source_target_pairs={{8,0},{16,8},{24,16},{32,24},{40,32},{48,40},{56,48},{64,56},{72,6... | collective-permute-start | bytes 393224 | tf_op jit(solution)/shard_map/ppermute | solution.py:23
  18.7 35.9 %collective-permute-start.3 = (f32[4,64,128]{2,1,0:T(8,128)S(1)}, f32[4,64,128]{2,1,0:T(8,128)S(1)}, u32[]{:S(2)}, u32[]{:S(2)}) collective-permute-start(f32[4,64,128]{2,1,0:T(8,128)S(1)} %get-tuple-element.69), channel_id=1, source_target_pairs={{0,8},{8,16},{16,24},{24,32},{32,40},{40,48},{48,56},{56,64},{64,7... | collective-permute-start | bytes 393224 | tf_op jit(solution)/shard_map/ppermute | solution.py:21
  30.6 24.0 %copy-start = (f32[16,64,128]{2,1,0:T(8,128)S(1)}, f32[16,64,128]{2,1,0:T(8,128)}, u32[]{:S(2)}) copy-start(f32[16,64,128]{2,1,0:T(8,128)} %param.16) | copy-start | bytes 1572868
  58.3 17.6 %copy-start.6 = (f32[16,64,128]{2,1,0:T(8,128)}, f32[16,64,128]{2,1,0:T(8,128)S(1)}, u32[]{:S(2)}) copy-start(f32[16,64,128]{2,1,0:T(8,128)S(1)} %get-tuple-element.61) | copy-start | bytes 1572868
  61.1 14.8 %collective-permute-start.10 = (f32[4,64,128]{2,1,0:T(8,128)S(1)}, f32[4,64,128]{2,1,0:T(8,128)S(1)}, u32[]{:S(2)}, u32[]{:S(2)}) collective-permute-start(f32[4,64,128]{2,1,0:T(8,128)S(1)} %get-tuple-element.59), channel_id=1, source_target_pairs={{8,0},{16,8},{24,16},{32,24},{40,32},{48,40},{56,48},{64,56},{72,6... | collective-permute-start | bytes 393224 | tf_op jit(solution)/shard_map/ppermute | solution.py:23
  63.0 12.9 %collective-permute-start.11 = (f32[4,64,128]{2,1,0:T(8,128)S(1)}, f32[4,64,128]{2,1,0:T(8,128)S(1)}, u32[]{:S(2)}, u32[]{:S(2)}) collective-permute-start(f32[4,64,128]{2,1,0:T(8,128)S(1)} %get-tuple-element.60), channel_id=1, source_target_pairs={{0,8},{8,16},{16,24},{24,32},{32,40},{40,48},{48,56},{56,64},{64,7... | collective-permute-start | bytes 393224 | tf_op jit(solution)/shard_map/ppermute | solution.py:21
  68.8 31.5 %collective-permute-start.4 = (f32[4,64,128]{2,1,0:T(8,128)}, f32[4,64,128]{2,1,0:T(8,128)S(1)}, u32[]{:S(2)}, u32[]{:S(2)}) collective-permute-start(f32[4,64,128]{2,1,0:T(8,128)} %get-tuple-element.66), channel_id=1, source_target_pairs={{8,0},{16,8},{24,16},{32,24},{40,32},{48,40},{56,48},{64,56},{72,6... | collective-permute-start | bytes 393224 | tf_op jit(solution)/shard_map/ppermute | solution.py:23
  70.7 29.6 %collective-permute-start.5 = (f32[4,64,128]{2,1,0:T(8,128)S(1)}, f32[4,64,128]{2,1,0:T(8,128)S(1)}, u32[]{:S(2)}, u32[]{:S(2)}) collective-permute-start(f32[4,64,128]{2,1,0:T(8,128)S(1)} %get-tuple-element.67), channel_id=1, source_target_pairs={{0,8},{8,16},{16,24},{24,32},{32,40},{40,48},{48,56},{56,64},{64,7... | collective-permute-start | bytes 393224 | tf_op jit(solution)/shard_map/ppermute | solution.py:21
  103.1 8.4 %copy-start.7 = (f32[16,64,128]{2,1,0:T(8,128)}, f32[16,64,128]{2,1,0:T(8,128)S(1)}, u32[]{:S(2)}) copy-start(f32[16,64,128]{2,1,0:T(8,128)S(1)} %get-tuple-element.58) | copy-start | bytes 1572868
  103.1 17.7 %collective-permute-start.12 = (f32[4,64,128]{2,1,0:T(8,128)S(1)}, f32[4,64,128]{2,1,0:T(8,128)S(1)}, u32[]{:S(2)}, u32[]{:S(2)}) collective-permute-start(f32[4,64,128]{2,1,0:T(8,128)S(1)} %get-tuple-element.56), channel_id=1, source_target_pairs={{8,0},{16,8},{24,16},{32,24},{40,32},{48,40},{56,48},{64,56},{72,6... | collective-permute-start | bytes 393224 | tf_op jit(solution)/shard_map/ppermute | solution.py:23
  105.0 15.8 %collective-permute-start.13 = (f32[4,64,128]{2,1,0:T(8,128)S(1)}, f32[4,64,128]{2,1,0:T(8,128)S(1)}, u32[]{:S(2)}, u32[]{:S(2)}) collective-permute-start(f32[4,64,128]{2,1,0:T(8,128)S(1)} %get-tuple-element.57), channel_id=1, source_target_pairs={{0,8},{8,16},{16,24},{24,32},{32,40},{40,48},{48,56},{56,64},{64,7... | collective-permute-start | bytes 393224 | tf_op jit(solution)/shard_map/ppermute | solution.py:21
  112.8 10.0 %copy-start.3 = (f32[16,64,128]{2,1,0:T(8,128)}, f32[16,64,128]{2,1,0:T(8,128)S(1)}, u32[]{:S(2)}) copy-start(f32[16,64,128]{2,1,0:T(8,128)S(1)} %scatter-add.45) | copy-start | bytes 1572868
  112.9 8.0 %copy-start.8 = (f32[16,64,128]{2,1,0:T(8,128)S(1)}, f32[16,64,128]{2,1,0:T(8,128)}, u32[]{:S(2)}) copy-start(f32[16,64,128]{2,1,0:T(8,128)} %copy-done.7) | copy-start | bytes 1572868
  113.6 24.5 %collective-permute-start.6 = (f32[4,64,128]{2,1,0:T(8,128)}, f32[4,64,128]{2,1,0:T(8,128)S(1)}, u32[]{:S(2)}, u32[]{:S(2)}) collective-permute-start(f32[4,64,128]{2,1,0:T(8,128)} %get-tuple-element.64), channel_id=1, source_target_pairs={{8,0},{16,8},{24,16},{32,24},{40,32},{48,40},{56,48},{64,56},{72,6... | collective-permute-start | bytes 393224 | tf_op jit(solution)/shard_map/ppermute | solution.py:23
  115.5 22.6 %collective-permute-start.7 = (f32[4,64,128]{2,1,0:T(8,128)}, f32[4,64,128]{2,1,0:T(8,128)}, u32[]{:S(2)}, u32[]{:S(2)}) collective-permute-start(f32[4,64,128]{2,1,0:T(8,128)} %get-tuple-element.65), channel_id=1, source_target_pairs={{0,8},{8,16},{16,24},{24,32},{32,40},{40,48},{48,56},{56,64},{64,7... | collective-permute-start | bytes 393224 | tf_op jit(solution)/shard_map/ppermute | solution.py:21
  148.7 9.4 %copy-start.4 = (f32[16,64,128]{2,1,0:T(8,128)}, f32[16,64,128]{2,1,0:T(8,128)S(1)}, u32[]{:S(2)}) copy-start(f32[16,64,128]{2,1,0:T(8,128)S(1)} %get-tuple-element.55) | copy-start | bytes 1572868
  148.7 19.5 %collective-permute-start.14 = (f32[4,64,128]{2,1,0:T(8,128)S(1)}, f32[4,64,128]{2,1,0:T(8,128)S(1)}, u32[]{:S(2)}, u32[]{:S(2)}) collective-permute-start(f32[4,64,128]{2,1,0:T(8,128)S(1)} %get-tuple-element.53), channel_id=1, source_target_pairs={{8,0},{16,8},{24,16},{32,24},{40,32},{48,40},{56,48},{64,56},{72,6... | collective-permute-start | bytes 393224 | tf_op jit(solution)/shard_map/ppermute | solution.py:23
  150.6 17.6 %collective-permute-start.15 = (f32[4,64,128]{2,1,0:T(8,128)S(1)}, f32[4,64,128]{2,1,0:T(8,128)}, u32[]{:S(2)}, u32[]{:S(2)}) collective-permute-start(f32[4,64,128]{2,1,0:T(8,128)S(1)} %get-tuple-element.54), channel_id=1, source_target_pairs={{0,8},{8,16},{16,24},{24,32},{32,40},{40,48},{48,56},{56,64},{64,7... | collective-permute-start | bytes 393224 | tf_op jit(solution)/shard_map/ppermute | solution.py:21
  159.5 8.7 %copy-start.5 = (f32[16,64,128]{2,1,0:T(8,128)S(1)}, f32[16,64,128]{2,1,0:T(8,128)}, u32[]{:S(2)}) copy-start(f32[16,64,128]{2,1,0:T(8,128)} %copy-done.4) | copy-start | bytes 1572868
  160.3 25.5 %collective-permute-start.8 = (f32[4,64,128]{2,1,0:T(8,128)}, f32[4,64,128]{2,1,0:T(8,128)S(1)}, u32[]{:S(2)}, u32[]{:S(2)}) collective-permute-start(f32[4,64,128]{2,1,0:T(8,128)} %get-tuple-element.62), channel_id=1, source_target_pairs={{8,0},{16,8},{24,16},{32,24},{40,32},{48,40},{56,48},{64,56},{72,6... | collective-permute-start | bytes 393224 | tf_op jit(solution)/shard_map/ppermute | solution.py:23
  162.2 23.6 %collective-permute-start.9 = (f32[4,64,128]{2,1,0:T(8,128)}, f32[4,64,128]{2,1,0:T(8,128)S(1)}, u32[]{:S(2)}, u32[]{:S(2)}) collective-permute-start(f32[4,64,128]{2,1,0:T(8,128)} %get-tuple-element.63), channel_id=1, source_target_pairs={{0,8},{8,16},{16,24},{24,32},{32,40},{40,48},{48,56},{56,64},{64,7... | collective-permute-start | bytes 393224 | tf_op jit(solution)/shard_map/ppermute | solution.py:21
  240.9 116.4 %copy-start.12 = (f32[16,8,128]{2,1,0:T(8,128)}, f32[16,8,128]{2,1,0:T(8,128)S(1)}, u32[]{:S(2)}) copy-start(f32[16,8,128]{2,1,0:T(8,128)S(1)} %broadcast_multiply_fusion) | copy-start | bytes 196612
  240.9 120.2 %copy-start.9 = (f32[2,5,16,8,128]{4,3,2,1,0:T(8,128)S(1)}, f32[2,5,16,8,128]{4,3,2,1,0:T(8,128)}, u32[]{:S(2)}) copy-start(f32[2,5,16,8,128]{4,3,2,1,0:T(8,128)} %param.25) | copy-start | bytes 1966084
  240.9 120.2 %copy-start.11 = (f32[16,8,128]{2,1,0:T(8,128)S(1)}, f32[16,8,128]{2,1,0:T(8,128)}, u32[]{:S(2)}) copy-start(f32[16,8,128]{2,1,0:T(8,128)} %reduce-scatter.2.cloned.1.call-done) | copy-start | bytes 196612
Sparse Core Ops, SparseCore 0:
  189.8 50.1 reduce-scatter.1

commit v2 on v0

v2 whole, which is shorter than its diff:
```python
import functools

import jax
import jax.numpy as jnp
from jax import lax
from jax.experimental import pallas as pl
from jax.experimental.pallas import tpu as pltpu
from jax.sharding import PartitionSpec as P

STEPS = 4
PAIRS = 5
REACH = 4
PAD = 8
MESH = pl.DeviceIdType.MESH

coefficients = (-205.0 / 72.0, 8.0 / 5.0, -1.0 / 5.0, 8.0 / 315.0, -1.0 / 560.0)


def kernel(
    depth_count,
    shot_count,
    inner_count,
    source_ref,
    wavelet_ref,
    receiver_ref,
    residual_ref,
    courant_hbm,
    before_hbm,
    current_hbm,
    after_hbm,
    adjoint_hbm,
    history_hbm,
    gradient_out,
    direction_out,
    next_out,
    wave,
    scaled_adj,
    lap,
    adj,
    before,
    after,
    courant,
    history,
    inject,
    terms,
    parts,
    gram,
    next_piece,
    slots_shot,
    slots_inner,
    slots_outer,
    load_sem,
    halo_send,
    halo_recv,
    part_send,
    part_recv,
    shot_send,
    shot_recv,
    inner_send,
    inner_recv,
    outer_send,
    outer_recv,
    next_send,
    next_recv,
    next_local,
):
    rows, width, lanes = courant.shape
    here = lax.axis_index("depth")
    me = lax.axis_index("shot")
    outer_count = depth_count // inner_count
    inner_me = lax.rem(here, inner_count)
    outer_me = lax.div(here, inner_count)
    piece = width // shot_count
    first = 0
    last = depth_count - 1

    def shot_peer(step):
        return lax.rem(me + step, shot_count)

    def inner_peer(step):
        return lax.rem(inner_me + step, inner_count)

    def outer_peer(step):
        return lax.rem(outer_me + step, outer_count)

    def depth_of(outer, inner):
        return outer * inner_count + inner

    barrier = pltpu.get_barrier_semaphore()

    def greet(depth, shot):
        pl.semaphore_signal(barrier, inc=1, device_id=(depth, shot), device_id_type=MESH)

    greet(lax.rem(here + 1, depth_count), me)
    greet(lax.rem(here + depth_count - 1, depth_count), me)
    for step in range(1, inner_count):
        greet(depth_of(outer_me, inner_peer(step)), me)
    for step in range(1, outer_count):
        greet(depth_of(outer_peer(step), inner_me), me)
    for step in range(1, shot_count):
        greet(here, shot_peer(step))
    greetings = 2 + (inner_count - 1) + (outer_count - 1) + (shot_count - 1)

    inside = pl.ds(REACH, rows)
    across = pl.ds(PAD, width)
    loads = [
        pltpu.make_async_copy(courant_hbm, courant, load_sem.at[0]),
        pltpu.make_async_copy(adjoint_hbm.at[0], adj.at[0], load_sem.at[1]),
        pltpu.make_async_copy(current_hbm.at[0], wave.at[0, inside, across], load_sem.at[2]),
        pltpu.make_async_copy(before_hbm.at[0], before, load_sem.at[3]),
        pltpu.make_async_copy(after_hbm.at[0], after, load_sem.at[4]),
        pltpu.make_async_copy(history_hbm, history, load_sem.at[5]),
    ]
    for load in loads:
        load.start()

    pads = jnp.zeros((rows, PAD, lanes), jnp.float32)
    for field in (wave, scaled_adj):
        for moment in range(STEPS):
            field[moment, pl.ds(REACH, rows), pl.ds(0, PAD), :] = pads
            field[moment, pl.ds(REACH, rows), pl.ds(PAD + width, PAD), :] = pads
    outside = jnp.zeros((REACH, width, lanes), jnp.float32)

    @pl.when(here == first)
    def _():
        for field in (wave, scaled_adj):
            for moment in range(STEPS):
                field[moment, pl.ds(0, REACH), across, :] = outside

    @pl.when(here == last)
    def _():
        for field in (wave, scaled_adj):
            for moment in range(STEPS):
                field[moment, pl.ds(REACH + rows, REACH), across, :] = outside

    def halo_copy(field, number, moment, up, source=None):
        if source is None:
            start = REACH if up else rows
            source = field.at[moment, pl.ds(start, REACH), across]
        target = field.at[moment, pl.ds(REACH + rows if up else 0, REACH), across]
        side = 0 if up else 1
        to = here - 1 if up else here + 1
        return pltpu.make_async_remote_copy(
            src_ref=source,
            dst_ref=target,
            send_sem=halo_send.at[number, moment, side],
            recv_sem=halo_recv.at[number, moment, side],
            device_id=(to, me),
            device_id_type=MESH,
        )

    def send_halo(field, number, moment, up, source=None):
        @pl.when(here > first if up else here < last)
        def _():
            halo_copy(field, number, moment, up, source).start()

    def wait_halo(field, number, moment, above):
        @pl.when(here > first if above else here < last)
        def _():
            halo_copy(field, number, moment, not above).wait_recv()

    pl.semaphore_wait(barrier, greetings)

    send_halo(wave, 0, 0, True, current_hbm.at[0, pl.ds(0, REACH)])
    send_halo(wave, 0, 0, False, current_hbm.at[0, pl.ds(rows - REACH, REACH)])

    loads[0].wait()
    loads[1].wait()

    def first_scaled(z):
        scaled_adj[0, z + REACH, across, :] = courant[z] * adj[0, z]

    def planes(low, high, body):
        def one(z, carry):
            body(z)
            return carry

        lax.fori_loop(low, high, one, 0)

    planes(0, REACH, first_scaled)
    send_halo(scaled_adj, 1, 0, True)
    planes(rows - REACH, rows, first_scaled)
    send_halo(scaled_adj, 1, 0, False)
    planes(REACH, rows - REACH, first_scaled)

    lane_bits = lanes.bit_length() - 1
    cells = receiver_ref[...]
    count = cells.shape[1]
    cell_rows = lax.shift_right_logical(cells, lane_bits) - here * (rows * width)
    cell_lanes = cells & (lanes - 1)
    lane_hit = lax.broadcasted_iota(jnp.int32, (lanes, count), 0) == cell_lanes
    block = 4 * width
    weights = []
    for moment in range(STEPS):
        value = jnp.where(lane_hit, residual_ref[0, moment : moment + 1, :], 0.0)
        high = value.astype(jnp.bfloat16)
        rest = value - high.astype(jnp.float32)
        middle = rest.astype(jnp.bfloat16)
        low = (rest - middle.astype(jnp.float32)).astype(jnp.bfloat16)
        weights.append((high, middle, low))

    def inject_block(number, carry):
        ids = lax.broadcasted_iota(jnp.int32, (block, count), 0) + number * block
        hit = jnp.where(ids == cell_rows, 1.0, 0.0).astype(jnp.bfloat16)
        for moment in range(STEPS):
            total = None
            for weight in reversed(weights[moment]):
                product = lax.dot_general(
                    hit, weight, (((1,), (1,)), ((), ())), preferred_element_type=jnp.float32
                )
                total = product if total is None else total + product
            inject[moment, pl.ds(number * 4, 4)] = total.reshape(4, width, lanes)
        return carry

    lax.fori_loop(0, rows // 4, inject_block, 0)

    source = source_ref[0]
    plane_ids = lax.broadcasted_iota(jnp.int32, (width, lanes), 0) * lanes
    plane_ids = plane_ids + lax.broadcasted_iota(jnp.int32, (width, lanes), 1)
    lane_ids = lax.broadcasted_iota(jnp.int32, (width, lanes), 1)

    def laplace(field, moment, z):
        at = z + REACH
        center = field[moment, at, across, :]
        total = (3.0 * coefficients[0]) * center
        for reach in range(1, REACH + 1):
            ahead = jnp.where(lane_ids < lanes - reach, pltpu.roll(center, lanes - reach, 1), 0.0)
            behind = jnp.where(lane_ids >= reach, pltpu.roll(center, reach, 1), 0.0)
            depth = field[moment, at + reach, across, :] + field[moment, at - reach, across, :]
            side = (
                field[moment, at, pl.ds(PAD + reach, width), :]
                + field[moment, at, pl.ds(PAD - reach, width), :]
            )
            total = total + coefficients[reach] * (depth + side + (ahead + behind))
        return center, total

    def forward_plane(moment, z):
        center, total = laplace(wave, moment, z)
        lap[moment, z] = total
        if moment < STEPS - 1:
            old = before[z] if moment == 0 else wave[moment - 1, z + REACH, across, :]
            new = 2.0 * center - old + courant[z] * total
            offset = source - (here * rows + z) * (width * lanes)
            new = new + jnp.where(plane_ids == offset, wavelet_ref[0, moment], 0.0)
            wave[moment + 1, z + REACH, across, :] = new

    def adjoint_plane(moment, z):
        _, total = laplace(scaled_adj, moment, z)
        old = after[z] if moment == 0 else adj[moment - 1, z]
        new = 2.0 * adj[moment, z] - old + total + inject[STEPS - 1 - moment, z]
        if moment < STEPS - 1:
            adj[moment + 1, z] = new
            scaled_adj[moment + 1, z + REACH, across, :] = courant[z] * new
        else:
            total = new * lap[0, z]
            for number in range(1, STEPS):
                total = total + adj[number, z] * lap[STEPS - number, z]
            terms[:, z] = total.reshape(shot_count, piece, lanes)

    stretches = ((REACH, rows - 2 * REACH), (0, REACH), (rows - REACH, REACH))

    def part_copy(number, peer, slot):
        start, length = stretches[number]
        return pltpu.make_async_remote_copy(
            src_ref=terms.at[peer, pl.ds(start, length)],
            dst_ref=parts.at[slot, pl.ds(start, length)],
            send_sem=part_send.at[number, peer],
            recv_sem=part_recv.at[number, slot],
            device_id=(here, peer),
            device_id_type=MESH,
        )

    def send_parts(number):
        for step in range(1, shot_count):
            part_copy(number, shot_peer(step), me).start()

    loads[2].wait()
    loads[3].wait()
    loads[4].wait()
    for moment in range(STEPS):
        more = moment < STEPS - 1
        planes(REACH, rows - REACH, functools.partial(forward_plane, moment))
        planes(REACH, rows - REACH, functools.partial(adjoint_plane, moment))
        if not more:
            send_parts(0)
        if moment == 0:
            loads[5].wait()
            pairs = [(0, i, j) for j in range(PAIRS) for i in range(j + 1)]
            pairs += [(1, i, j) for j in range(PAIRS) for i in range(j + 1)]

            def gram_plane(z, sums):
                held = [[history[kind, i, z] for i in range(PAIRS)] for kind in range(2)]
                return tuple(
                    total + held[kind][i] * held[1][j]
                    for total, (kind, i, j) in zip(sums, pairs)
                )

            sums = lax.fori_loop(
                0, rows, gram_plane, tuple(jnp.zeros((piece, lanes), jnp.float32) for _ in pairs)
            )
            row_lane = lax.broadcasted_iota(jnp.int32, (1, lanes), 1)
            packed = jnp.zeros((1, lanes), jnp.float32)
            for total, (kind, i, j) in zip(sums, pairs):
                value = jnp.sum(jnp.sum(total, axis=0, keepdims=True), axis=1, keepdims=True)
                spots = [(2 + PAIRS * kind + j) * 8 + i]
                if kind == 1 and i != j:
                    spots.append((2 + PAIRS * kind + i) * 8 + j)
                for spot in spots:
                    packed = jnp.where(row_lane == spot, value, packed)
            gram[...] = packed
        wait_halo(wave, 0, moment, True)
        planes(0, REACH, functools.partial(forward_plane, moment))
        if more:
            send_halo(wave, 0, moment + 1, True)
        wait_halo(wave, 0, moment, False)
        planes(rows - REACH, rows, functools.partial(forward_plane, moment))
        if more:
            send_halo(wave, 0, moment + 1, False)
        wait_halo(scaled_adj, 1, moment, True)
        planes(0, REACH, functools.partial(adjoint_plane, moment))
        if more:
            send_halo(scaled_adj, 1, moment + 1, True)
        else:
            send_parts(1)
        wait_halo(scaled_adj, 1, moment, False)
        planes(rows - REACH, rows, functools.partial(adjoint_plane, moment))
        if more:
            send_halo(scaled_adj, 1, moment + 1, False)
        else:
            send_parts(2)

    for number in range(len(stretches)):
        for step in range(1, shot_count):
            part_copy(number, me, shot_peer(step)).wait_recv()

    scale = 1.0 / (shot_count * STEPS)

    def own_plane(z, sums):
        total = terms[me, z]
        for step in range(1, shot_count):
            total = total + parts[shot_peer(step), z]
        total = total * scale
        gradient_out[z] = total
        return tuple(
            held + history[number // PAIRS, number % PAIRS, z] * total
            for number, held in enumerate(sums)
        )

    sums = lax.fori_loop(
        0, rows, own_plane, tuple(jnp.zeros((piece, lanes), jnp.float32) for _ in range(2 * PAIRS))
    )
    row_lane = lax.broadcasted_iota(jnp.int32, (1, lanes), 1)
    packed = gram[...]
    for number, total in enumerate(sums):
        value = jnp.sum(jnp.sum(total, axis=0, keepdims=True), axis=1, keepdims=True)
        spot = (number // PAIRS) * 8 + number % PAIRS
        packed = jnp.where(row_lane == spot, value, packed)

    def gather_sum(value, slots, send, recv, mine, number, peer_of, device_of):
        slots[mine] = value

        def one(peer, slot):
            return pltpu.make_async_remote_copy(
                src_ref=slots.at[mine],
                dst_ref=slots.at[slot],
                send_sem=send.at[peer],
                recv_sem=recv.at[slot],
                device_id=device_of(peer),
                device_id_type=MESH,
            )

        for step in range(1, number):
            one(peer_of(step), mine).start()
        for step in range(1, number):
            one(mine, peer_of(step)).wait_recv()
        total = slots[0]
        for slot in range(1, number):
            total = total + slots[slot]
        for step in range(1, number):
            one(peer_of(step), mine).wait_send()
        return total

    packed = gather_sum(
        packed, slots_shot, shot_send, shot_recv, me, shot_count,
        shot_peer, lambda peer: (here, peer),
    )
    packed = gather_sum(
        packed, slots_inner, inner_send, inner_recv, inner_me, inner_count,
        inner_peer, lambda peer: (depth_of(outer_me, peer), me),
    )
    packed = gather_sum(
        packed, slots_outer, outer_send, outer_recv, outer_me, outer_count,
        outer_peer, lambda peer: (depth_of(peer, inner_me), me),
    )

    spread = jnp.broadcast_to(packed, (8, lanes))
    sub = lax.broadcasted_iota(jnp.int32, (8, lanes), 0)
    lane = lax.broadcasted_iota(jnp.int32, (8, lanes), 1)

    def column(spots):
        return jnp.broadcast_to(
            jnp.sum(jnp.where(lane == spots, spread, 0.0), axis=1, keepdims=True), (8, lanes)
        )

    step_grad = column(sub)
    change_grad = column(8 + sub)
    step_change = [column((2 + j) * 8 + sub) for j in range(PAIRS)]
    step_change_row = [column((2 + sub) * 8 + i) for i in range(PAIRS)]
    change_change = [column((2 + PAIRS + j) * 8 + sub) for j in range(PAIRS)]
    curvature = jnp.where(sub < PAIRS, column((2 + sub) * 8 + sub), 1.0)
    inverse = 1.0 / curvature

    def entry(value, i):
        return jnp.broadcast_to(value[i : i + 1, :], (8, lanes))

    alphas = [None] * PAIRS
    running = step_grad
    for i in reversed(range(PAIRS)):
        alphas[i] = entry(inverse * running, i)
        running = running - alphas[i] * step_change[i]
    gamma = entry(curvature, PAIRS - 1) / entry(change_change[PAIRS - 1], PAIRS - 1)
    running = change_grad
    for j in range(PAIRS):
        running = running - alphas[j] * change_change[j]
    running = gamma * running
    gains = []
    for i in range(PAIRS):
        gain = alphas[i] - entry(inverse * running, i)
        gains.append(gain)
        running = running + gain * step_change_row[i]

    own_lateral = pl.ds(pl.multiple_of(me * piece, piece), piece)

    def direction_plane(z, carry):
        search = gradient_out[z]
        for i in range(PAIRS):
            search = search - alphas[i] * history[1, i, z]
        search = gamma * search
        for i in range(PAIRS):
            search = search + gains[i] * history[0, i, z]
        direction_out[z] = -search
        next_piece[z] = courant[z, own_lateral, :] - 0.05 * search
        return carry

    lax.fori_loop(0, rows, direction_plane, 0)

    def next_copy(peer, slot):
        spot = pl.ds(pl.multiple_of(slot * piece, piece), piece)
        return pltpu.make_async_remote_copy(
            src_ref=next_piece,
            dst_ref=next_out.at[:, spot],
            send_sem=next_send.at[peer],
            recv_sem=next_recv.at[slot],
            device_id=(here, peer),
            device_id_type=MESH,
        )

    for step in range(1, shot_count):
        next_copy(shot_peer(step), me).start()
    own = pltpu.make_async_copy(next_piece, next_out.at[:, own_lateral], next_local)
    own.start()

    for number, field in enumerate((wave, scaled_adj)):
        for moment in range(STEPS):
            for up in (True, False):

                @pl.when(here > first if up else here < last)
                def _():
                    halo_copy(field, number, moment, up).wait_send()

    for number in range(len(stretches)):
        for step in range(1, shot_count):
            part_copy(number, shot_peer(step), me).wait_send()
    own.wait()
    for step in range(1, shot_count):
        next_copy(me, shot_peer(step)).wait_recv()
    for step in range(1, shot_count):
        next_copy(shot_peer(step), me).wait_send()


def per_device(
    courant,
    wave_before,
    wave_current,
    adjoint_after,
    adjoint_current,
    source_cell,
    wavelet,
    receiver_cell,
    residual,
    history,
):
    depth_count = lax.axis_size("depth")
    shot_count = lax.axis_size("shot")
    inner_count = 4
    outer_count = depth_count // inner_count
    rows, width, lanes = courant.shape
    piece = width // shot_count
    f32 = jnp.float32
    slab = (rows, width, lanes)
    padded = (STEPS, rows + 2 * REACH, width + 2 * PAD, lanes)
    vmem = pl.BlockSpec(memory_space=pltpu.VMEM)
    smem = pl.BlockSpec(memory_space=pltpu.SMEM)
    anywhere = pl.BlockSpec(memory_space=pltpu.HBM)
    dma = pltpu.SemaphoreType.DMA
    return pl.pallas_call(
        functools.partial(kernel, depth_count, shot_count, inner_count),
        out_shape=(
            jax.ShapeDtypeStruct((rows, piece, lanes), f32),
            jax.ShapeDtypeStruct((rows, piece, lanes), f32),
            jax.ShapeDtypeStruct(slab, f32),
        ),
        in_specs=[smem, smem, vmem, vmem] + [anywhere] * 6,
        out_specs=(vmem, vmem, anywhere),
        scratch_shapes=[
            pltpu.VMEM(padded, f32),
            pltpu.VMEM(padded, f32),
            pltpu.VMEM((STEPS,) + slab, f32),
            pltpu.VMEM((STEPS,) + slab, f32),
            pltpu.VMEM(slab, f32),
            pltpu.VMEM(slab, f32),
            pltpu.VMEM(slab, f32),
            pltpu.VMEM(history.shape, f32),
            pltpu.VMEM((STEPS,) + slab, f32),
            pltpu.VMEM((shot_count, rows, piece, lanes), f32),
            pltpu.VMEM((shot_count, rows, piece, lanes), f32),
            pltpu.VMEM((1, lanes), f32),
            pltpu.VMEM((rows, piece, lanes), f32),
            pltpu.VMEM((shot_count, 1, lanes), f32),
            pltpu.VMEM((inner_count, 1, lanes), f32),
            pltpu.VMEM((outer_count, 1, lanes), f32),
            dma((6,)),
            dma((2, STEPS, 2)),
            dma((2, STEPS, 2)),
            dma((3, shot_count)),
            dma((3, shot_count)),
            dma((shot_count,)),
            dma((shot_count,)),
            dma((inner_count,)),
            dma((inner_count,)),
            dma((outer_count,)),
            dma((outer_count,)),
            dma((shot_count,)),
            dma((shot_count,)),
            dma,
        ],
        compiler_params=pltpu.CompilerParams(
            collective_id=0, has_side_effects=True, vmem_limit_bytes=56 * 1024 * 1024
        ),
    )(
        source_cell,
        wavelet,
        receiver_cell,
        residual,
        courant,
        wave_before,
        wave_current,
        adjoint_after,
        adjoint_current,
        history,
    )


def solution(mesh):
    return jax.shard_map(
        per_device,
        mesh=mesh,
        in_specs=(
            P("depth", None, None),
            P("shot", "depth", None, None),
            P("shot", "depth", None, None),
            P("shot", "depth", None, None),
            P("shot", "depth", None, None),
            P("shot"),
            P("shot", None),
            P("shot", None),
            P("shot", None, None),
            P(None, None, "depth", "shot", None),
        ),
        out_specs=(P("depth", "shot", None), P("depth", "shot", None), P("depth", None, None)),
        check_vma=False,
    )
```

time: 1060 us -> 73.4 us (0.07); the launches traced: 1050 us -> 73.2 us
  blocking collectives: 767 us -> 0 us
  other arithmetic: 123 us -> 0 us
  Pallas kernels: 0 us -> 67.9 us
  starting transfers between devices: 59.8 us -> 0 us
  waiting for transfers between devices: 50.2 us -> 0 us
  between operations: 37.1 us -> 1.3 us
    psum x10 -> x0, blocking collectives: 743 us -> none  [the longest x5 369 us: per_device(): lax.psum(jnp.sum(changes[number] * scaled), ('depth', 'shot'))]
    scatter-add x4 -> x0, other arithmetic: 69.7 us -> none  [inject(): volume.at[row_safe, remainder // volume.shape[2], remainder % volume.shap...]
    pallas_call x0 -> x1, Pallas kernels: none -> 67.9 us  [per_device(): pl.pallas_call(functools.partial(kernel, depth_count, shot_count, inner_c...]
    ppermute x16 -> x0, starting transfers between devices: 59.7 us -> none  [the longest x8 41.1 us: with_halo(): lax.ppermute(tail, axis, [(i, (i + 1) % count) for i in range(ends)])]
    reduce_scatter x1 -> x0, waiting for transfers between devices: 50.1 us -> none  [per_device(): lax.psum_scatter(summed, 'shot', scatter_dimension=1, tiled=True)]
    add x9 -> x0, other arithmetic: 43.2 us -> none  [the longest x3 17.3 us: per_device(): wave_new = 2.0 * wave_now - wave_old + courant * laplacian]
    all_gather x1 -> x0, blocking collectives: 24.3 us -> none  [per_device(): courant_next = lax.all_gather(next_piece, 'shot', axis=1, tiled=True)]
  transfers between devices with their start and end apart: 17 -> 0, of which waited for: 1 -> 0; matrix products, arithmetic and copies ran while one was open for 9% -> 0% of each run, Pallas kernels for 0% -> 0%
where the time goes in v2:
time: 73.4 us; the launch traced here: 73.2 us
  Pallas kernels  67.9 us (93%)
  local copies, waits for them, and re-layouts  4.02 us (5%)
  between operations  1.3 us (2%)
    pallas_call x1, Pallas kernels, per_device(): pl.pallas_call(functools.partial(kernel, depth_count, shot_count, inner_c...  67.9 us
    unnamed x5, local copies, waits for them, and re-layouts  4.02 us

profile of v2, /device:TPU:1, one launch (start us, length us, event | category | flops | bytes accessed | tf_op | source)
XLA Modules:
  0.0 73.2 jit_solution(7319694223102103306)
XLA Ops:
  1.3 67.9 %shard_map.121 = (f32[16,8,128]{2,1,0:T(8,128)}, f32[16,8,128]{2,1,0:T(8,128)}, f32[16,64,128]{2,1,0:T(8,128)}) custom-call(s32[1]{0:T(128)S(6)} %copy.16.source_ref, f32[1,4]{1,0:T(1,128)} %wavelet_ref.1, s32[1,256]{1,0:T(1,128)} %receiver_ref.1, f32[1,4,256]{2,1,0:T(4,128)} %residual_ref.1, f32[16,64,128]{2,1,0:T(8,128)} %courant_hbm.1, ...), custom_call_target="tpu_custom_call" | custom-call | tf_op jit(solution)/shard_map/pallas_call | solution.py:506
  69.2 0.0 copy-start
  69.2 1.5 %copy.17 = f32[16,8,128]{2,1,0:T(8,128)} copy(f32[16,8,128]{2,1,0:T(8,128)} %get-tuple-element.6) | data formatting | bytes 131072
  70.7 0.0 copy-done
  70.7 0.6 copy.18
  71.3 1.9 %copy.19 = f32[16,64,128]{2,1,0:T(8,128)} copy(f32[16,64,128]{2,1,0:T(8,128)} %get-tuple-element.8) | data formatting | bytes 1048576
Async XLA Ops:
  69.2 1.5 %copy-start = (f32[16,8,128]{2,1,0:T(8,128)S(1)}, f32[16,8,128]{2,1,0:T(8,128)}, u32[]{:S(2)}) copy-start(f32[16,8,128]{2,1,0:T(8,128)} %get-tuple-element.7) | copy-start | bytes 196612

commit v3 on v2

--- a/solution.py
+++ b/solution.py
@@ -10,10 +10,20 @@
 STEPS = 4
 PAIRS = 5
 REACH = 4
+BLOCK = 4
 PAD = 8
+DENOMINATOR = 5040
 MESH = pl.DeviceIdType.MESH
 
 coefficients = (-205.0 / 72.0, 8.0 / 5.0, -1.0 / 5.0, 8.0 / 315.0, -1.0 / 560.0)
+
+
+def in_three(value):
+    high = value.astype(jnp.bfloat16)
+    rest = value - high.astype(jnp.float32)
+    middle = rest.astype(jnp.bfloat16)
+    low = (rest - middle.astype(jnp.float32)).astype(jnp.bfloat16)
+    return high, middle, low
 
 
 def kernel(
@@ -21,9 +31,9 @@
     shot_count,
     inner_count,
     source_ref,
-    wavelet_ref,
-    receiver_ref,
-    residual_ref,
+    wavelet_hbm,
+    receiver_hbm,
+    residual_hbm,
     courant_hbm,
     before_hbm,
     current_hbm,
@@ -33,6 +43,9 @@
     gradient_out,
     direction_out,
     next_out,
+    wavelet_ref,
+    receiver_ref,
+    residual_ref,
     wave,
     scaled_adj,
     lap,
@@ -46,18 +59,17 @@
     parts,
     gram,
     next_piece,
-    slots_shot,
-    slots_inner,
+    band,
+    lateral,
+    slots_near,
     slots_outer,
     load_sem,
     halo_send,
     halo_recv,
     part_send,
     part_recv,
-    shot_send,
-    shot_recv,
-    inner_send,
-    inner_recv,
+    near_send,
+    near_recv,
     outer_send,
     outer_recv,
     next_send,
@@ -77,9 +89,6 @@
     def shot_peer(step):
         return lax.rem(me + step, shot_count)
 
-    def inner_peer(step):
-        return lax.rem(inner_me + step, inner_count)
-
     def outer_peer(step):
         return lax.rem(outer_me + step, outer_count)
 
@@ -91,15 +100,37 @@
     def greet(depth, shot):
         pl.semaphore_signal(barrier, inc=1, device_id=(depth, shot), device_id_type=MESH)
 
+    half = shot_count // 2
+    order = [
+        (turn, flip, chip, core)
+        for turn in range(half)
+        for flip in range(2)
+        for chip in range(inner_count // 2)
+        for core in range(2)
+    ]
+    order.remove((0, 0, 0, 0))
+
+    def hops(offset):
+        turn, flip, chip, core = offset
+        return min(turn, half - turn) + (1 if flip else 2 * chip) + 0.1 * core
+
+    order.sort(key=hops, reverse=True)
+
+    def near_peer(offset):
+        turn, flip, chip, core = offset
+        shot = lax.rem(lax.div(me, 2) + turn, half) * 2 + lax.rem(lax.rem(me, 2) + flip, 2)
+        inner = lax.rem(lax.div(inner_me, 2) + chip, inner_count // 2) * 2
+        inner = inner + lax.rem(lax.rem(inner_me, 2) + core, 2)
+        return depth_of(outer_me, inner), shot
+
+    near_peers = [near_peer(offset) for offset in order]
+    turns = sorted(range(1, outer_count), key=lambda turn: -min(turn, outer_count - turn))
+    outer_peers = [(depth_of(outer_peer(turn), inner_me), me) for turn in turns]
+    for depth, shot in outer_peers + near_peers:
+        greet(depth, shot)
     greet(lax.rem(here + 1, depth_count), me)
     greet(lax.rem(here + depth_count - 1, depth_count), me)
-    for step in range(1, inner_count):
-        greet(depth_of(outer_me, inner_peer(step)), me)
-    for step in range(1, outer_count):
-        greet(depth_of(outer_peer(step), inner_me), me)
-    for step in range(1, shot_count):
-        greet(here, shot_peer(step))
-    greetings = 2 + (inner_count - 1) + (outer_count - 1) + (shot_count - 1)
+    greetings = 2 + len(near_peers) + len(outer_peers)
 
     inside = pl.ds(REACH, rows)
     across = pl.ds(PAD, width)
@@ -110,6 +141,9 @@
         pltpu.make_async_copy(before_hbm.at[0], before, load_sem.at[3]),
         pltpu.make_async_copy(after_hbm.at[0], after, load_sem.at[4]),
         pltpu.make_async_copy(history_hbm, history, load_sem.at[5]),
+        pltpu.make_async_copy(receiver_hbm, receiver_ref, load_sem.at[6]),
+        pltpu.make_async_copy(residual_hbm, residual_ref, load_sem.at[7]),
+        pltpu.make_async_copy(wavelet_hbm, wavelet_ref, load_sem.at[8]),
     ]
     for load in loads:
         load.start()
@@ -184,6 +218,8 @@
     planes(REACH, rows - REACH, first_scaled)
 
     lane_bits = lanes.bit_length() - 1
+    for load in loads[6:]:
+        load.wait()
     cells = receiver_ref[...]
     count = cells.shape[1]
     cell_rows = lax.shift_right_logical(cells, lane_bits) - here * (rows * width)
@@ -193,11 +229,7 @@
     weights = []
     for moment in range(STEPS):
         value = jnp.where(lane_hit, residual_ref[0, moment : moment + 1, :], 0.0)
-        high = value.astype(jnp.bfloat16)
-        rest = value - high.astype(jnp.float32)
-        middle = rest.astype(jnp.bfloat16)
-        low = (rest - middle.astype(jnp.float32)).astype(jnp.bfloat16)
-        weights.append((high, middle, low))
+        weights.append(in_three(value))
 
     def inject_block(number, carry):
         ids = lax.broadcasted_iota(jnp.int32, (block, count), 0) + number * block
@@ -217,21 +249,35 @@
     source = source_ref[0]
     plane_ids = lax.broadcasted_iota(jnp.int32, (width, lanes), 0) * lanes
     plane_ids = plane_ids + lax.broadcasted_iota(jnp.int32, (width, lanes), 1)
-    lane_ids = lax.broadcasted_iota(jnp.int32, (width, lanes), 1)
+
+    gap = jnp.abs(
+        lax.broadcasted_iota(jnp.int32, (lanes, lanes), 0)
+        - lax.broadcasted_iota(jnp.int32, (lanes, lanes), 1)
+    )
+    weight = jnp.zeros((lanes, lanes), jnp.float32)
+    for reach in range(1, REACH + 1):
+        weight = jnp.where(gap == reach, float(round(DENOMINATOR * coefficients[reach])), weight)
+    weight = weight.astype(jnp.bfloat16)
+    for number in range(3):
+        band[pl.ds(number * lanes, lanes), :] = weight
+
+    def along(field, moment, low, count):
+        value = field[moment, pl.ds(low + REACH, count), across, :].reshape(count * width, lanes)
+        split = jnp.concatenate(in_three(value), axis=1)
+        product = jnp.dot(split, band[...], preferred_element_type=jnp.float32)
+        lateral[pl.ds(low, count)] = product.reshape(count, width, lanes)
 
     def laplace(field, moment, z):
         at = z + REACH
         center = field[moment, at, across, :]
-        total = (3.0 * coefficients[0]) * center
+        total = (3.0 * coefficients[0]) * center + (1.0 / DENOMINATOR) * lateral[z]
         for reach in range(1, REACH + 1):
-            ahead = jnp.where(lane_ids < lanes - reach, pltpu.roll(center, lanes - reach, 1), 0.0)
-            behind = jnp.where(lane_ids >= reach, pltpu.roll(center, reach, 1), 0.0)
             depth = field[moment, at + reach, across, :] + field[moment, at - reach, across, :]
             side = (
                 field[moment, at, pl.ds(PAD + reach, width), :]
                 + field[moment, at, pl.ds(PAD - reach, width), :]
             )
-            total = total + coefficients[reach] * (depth + side + (ahead + behind))
+            total = total + coefficients[reach] * (depth + side)
         return center, total
 
     def forward_plane(moment, z):
@@ -274,14 +320,24 @@
         for step in range(1, shot_count):
             part_copy(number, shot_peer(step), me).start()
 
+    def forward(moment, low, high):
+        for start in range(low, high, BLOCK):
+            along(wave, moment, start, BLOCK)
+        planes(low, high, functools.partial(forward_plane, moment))
+
+    def adjoint(moment, low, high):
+        for start in range(low, high, BLOCK):
+            along(scaled_adj, moment, start, BLOCK)
+        planes(low, high, functools.partial(adjoint_plane, moment))
+
     loads[2].wait()
     loads[3].wait()
     loads[4].wait()
     for moment in range(STEPS):
         more = moment < STEPS - 1
-        planes(REACH, rows - REACH, functools.partial(forward_plane, moment))
-        planes(REACH, rows - REACH, functools.partial(adjoint_plane, moment))
+        forward(moment, REACH, rows - REACH)
         if not more:
+            adjoint(moment, REACH, rows - REACH)
             send_parts(0)
         if moment == 0:
             loads[5].wait()
@@ -309,21 +365,23 @@
                     packed = jnp.where(row_lane == spot, value, packed)
             gram[...] = packed
         wait_halo(wave, 0, moment, True)
-        planes(0, REACH, functools.partial(forward_plane, moment))
+        forward(moment, 0, REACH)
         if more:
             send_halo(wave, 0, moment + 1, True)
         wait_halo(wave, 0, moment, False)
-        planes(rows - REACH, rows, functools.partial(forward_plane, moment))
+        forward(moment, rows - REACH, rows)
         if more:
             send_halo(wave, 0, moment + 1, False)
+        if more:
+            adjoint(moment, REACH, rows - REACH)
         wait_halo(scaled_adj, 1, moment, True)
-        planes(0, REACH, functools.partial(adjoint_plane, moment))
+        adjoint(moment, 0, REACH)
         if more:
             send_halo(scaled_adj, 1, moment + 1, True)
         else:
             send_parts(1)
         wait_halo(scaled_adj, 1, moment, False)
-        planes(rows - REACH, rows, functools.partial(adjoint_plane, moment))
+        adjoint(moment, rows - REACH, rows)
         if more:
             send_halo(scaled_adj, 1, moment + 1, False)
         else:
@@ -356,42 +414,36 @@
         spot = (number // PAIRS) * 8 + number % PAIRS
         packed = jnp.where(row_lane == spot, value, packed)
 
-    def gather_sum(value, slots, send, recv, mine, number, peer_of, device_of):
+    def gather_sum(value, slots, send, recv, mine, peers):
         slots[mine] = value
-
-        def one(peer, slot):
-            return pltpu.make_async_remote_copy(
+        for peer in peers:
+            pltpu.make_async_remote_copy(
                 src_ref=slots.at[mine],
-                dst_ref=slots.at[slot],
-                send_sem=send.at[peer],
-                recv_sem=recv.at[slot],
-                device_id=device_of(peer),
+                dst_ref=slots.at[mine],
+                send_sem=send,
+                recv_sem=recv,
+                device_id=peer,
                 device_id_type=MESH,
-            )
-
-        for step in range(1, number):
-            one(peer_of(step), mine).start()
-        for step in range(1, number):
-            one(mine, peer_of(step)).wait_recv()
-        total = slots[0]
-        for slot in range(1, number):
-            total = total + slots[slot]
-        for step in range(1, number):
-            one(peer_of(step), mine).wait_send()
-        return total
-
-    packed = gather_sum(
-        packed, slots_shot, shot_send, shot_recv, me, shot_count,
-        shot_peer, lambda peer: (here, peer),
-    )
-    packed = gather_sum(
-        packed, slots_inner, inner_send, inner_recv, inner_me, inner_count,
-        inner_peer, lambda peer: (depth_of(outer_me, peer), me),
-    )
-    packed = gather_sum(
-        packed, slots_outer, outer_send, outer_recv, outer_me, outer_count,
-        outer_peer, lambda peer: (depth_of(peer, inner_me), me),
-    )
+            ).start()
+        every = slots.at[pl.ds(0, len(peers))]
+        every = pltpu.make_async_remote_copy(
+            src_ref=every,
+            dst_ref=every,
+            send_sem=send,
+            recv_sem=recv,
+            device_id=peers[0],
+            device_id_type=MESH,
+        )
+        every.wait_recv()
+        sums = [slots[slot] for slot in range(len(peers) + 1)]
+        while len(sums) > 1:
+            sums = [sums[i] + sums[i + 1] for i in range(0, len(sums), 2)]
+        every.wait_send()
+        return sums[0]
+
+    near_me = me * inner_count + inner_me
+    packed = gather_sum(packed, slots_near, near_send, near_recv, near_me, near_peers)
+    packed = gather_sum(packed, slots_outer, outer_send, outer_recv, outer_me, outer_peers)
 
     spread = jnp.broadcast_to(packed, (8, lanes))
     sub = lax.broadcasted_iota(jnp.int32, (8, lanes), 0)
@@ -500,7 +552,6 @@
     slab = (rows, width, lanes)
     padded = (STEPS, rows + 2 * REACH, width + 2 * PAD, lanes)
     vmem = pl.BlockSpec(memory_space=pltpu.VMEM)
-    smem = pl.BlockSpec(memory_space=pltpu.SMEM)
     anywhere = pl.BlockSpec(memory_space=pltpu.HBM)
     dma = pltpu.SemaphoreType.DMA
     return pl.pallas_call(
@@ -510,9 +561,12 @@
             jax.ShapeDtypeStruct((rows, piece, lanes), f32),
             jax.ShapeDtypeStruct(slab, f32),
         ),
-        in_specs=[smem, smem, vmem, vmem] + [anywhere] * 6,
+        in_specs=[pl.BlockSpec(memory_space=pltpu.SMEM)] + [anywhere] * 9,
         out_specs=(vmem, vmem, anywhere),
         scratch_shapes=[
+            pltpu.SMEM(wavelet.shape, f32),
+            pltpu.VMEM(receiver_cell.shape, jnp.int32),
+            pltpu.VMEM(residual.shape, f32),
             pltpu.VMEM(padded, f32),
             pltpu.VMEM(padded, f32),
             pltpu.VMEM((STEPS,) + slab, f32),
@@ -526,38 +580,42 @@
             pltpu.VMEM((shot_count, rows, piece, lanes), f32),
             pltpu.VMEM((1, lanes), f32),
             pltpu.VMEM((rows, piece, lanes), f32),
-            pltpu.VMEM((shot_count, 1, lanes), f32),
-            pltpu.VMEM((inner_count, 1, lanes), f32),
+            pltpu.VMEM((3 * lanes, lanes), jnp.bfloat16),
+            pltpu.VMEM(slab, f32),
+            pltpu.VMEM((shot_count * inner_count, 1, lanes), f32),
             pltpu.VMEM((outer_count, 1, lanes), f32),
-            dma((6,)),
+            dma((9,)),
             dma((2, STEPS, 2)),
             dma((2, STEPS, 2)),
             dma((3, shot_count)),
             dma((3, shot_count)),
-            dma((shot_count,)),
-            dma((shot_count,)),
-            dma((inner_count,)),
-            dma((inner_count,)),
-            dma((outer_count,)),
-            dma((outer_count,)),
+            dma,
+            dma,
+            dma,
+            dma,
             dma((shot_count,)),
             dma((shot_count,)),
             dma,
         ],
         compiler_params=pltpu.CompilerParams(
-            collective_id=0, has_side_effects=True, vmem_limit_bytes=56 * 1024 * 1024
+            collective_id=0, has_side_effects=True, vmem_limit_bytes=36 * 1024 * 1024
         ),
     )(
         source_cell,
-        wavelet,
-        receiver_cell,
-        residual,
-        courant,
-        wave_before,
-        wave_current,
-        adjoint_after,
-        adjoint_current,
-        history,
+        *(
+            pltpu.with_memory_space_constraint(array, pltpu.HBM)
+            for array in (
+                wavelet,
+                receiver_cell,
+                residual,
+                courant,
+                wave_before,
+                wave_current,
+                adjoint_after,
+                adjoint_current,
+                history,
+            )
+        )
     )
 
 

time: 73.4 us -> 66.4 us (0.905)
  Pallas kernels: 67.9 us -> 63 us
  local copies, waits for them, and re-layouts: 4.02 us -> 2.05 us
    pallas_call x1, Pallas kernels: 67.9 us -> 63 us  [per_device(): pl.pallas_call(functools.partial(kernel, depth_count, shot_count, inner_c...]
    unnamed x5 -> x3, local copies, waits for them, and re-layouts: 4.02 us -> 2.05 us
where the time goes in v3:
time: 66.4 us; the launch traced here: 66.3 us
  Pallas kernels  63 us (95%)
  local copies, waits for them, and re-layouts  2.05 us (3%)
  between operations  1.29 us (2%)
    pallas_call x1, Pallas kernels, per_device(): pl.pallas_call(functools.partial(kernel, depth_count, shot_count, inner_c...  63 us
    unnamed x3, local copies, waits for them, and re-layouts  2.05 us

profile of v3, /device:TPU:1, one launch (start us, length us, event | category | flops | bytes accessed | tf_op | source)
XLA Modules:
  0.0 66.3 jit_solution(2204787483740456612)
XLA Ops:
  1.3 63.0 %shard_map.121 = (f32[16,8,128]{2,1,0:T(8,128)S(1)}, f32[16,8,128]{2,1,0:T(8,128)S(1)}, f32[16,64,128]{2,1,0:T(8,128)S(1)}) custom-call(s32[1]{0:T(128)S(6)} %copy.16.source_ref, f32[1,4]{1,0:T(1,128)} %wavelet_hbm.1, s32[1,256]{1,0:T(1,128)} %receiver_hbm.1, f32[1,4,256]{2,1,0:T(4,128)} %residual_hbm.1, f32[16,64,128]{2,1,0:T(8,128)} %courant_hbm.1, ...), custom_call_target="tpu_custom_call" | custom-call | tf_op jit(solution)/shard_map/pallas_call | solution.py:557
  64.3 0.6 copy.17
  64.9 0.6 copy.18
  65.5 0.8 %copy.19 = f32[16,64,128]{2,1,0:T(8,128)} copy(f32[16,64,128]{2,1,0:T(8,128)S(1)} %get-tuple-element.8) | data formatting | bytes 1048576

commit v4 on v3

--- a/solution.py
+++ b/solution.py
@@ -40,8 +40,7 @@
     after_hbm,
     adjoint_hbm,
     history_hbm,
-    gradient_out,
-    direction_out,
+    pair_out,
     next_out,
     wavelet_ref,
     receiver_ref,
@@ -124,12 +123,16 @@
         return depth_of(outer_me, inner), shot
 
     near_peers = [near_peer(offset) for offset in order]
+    shot_order = sorted(
+        range(1, shot_count),
+        key=lambda step: (step % 2 == 0, abs(step - half - (step % 2))),
+    )
     turns = sorted(range(1, outer_count), key=lambda turn: -min(turn, outer_count - turn))
     outer_peers = [(depth_of(outer_peer(turn), inner_me), me) for turn in turns]
+    greet(lax.rem(here + 1, depth_count), me)
+    greet(lax.rem(here + depth_count - 1, depth_count), me)
     for depth, shot in outer_peers + near_peers:
         greet(depth, shot)
-    greet(lax.rem(here + 1, depth_count), me)
-    greet(lax.rem(here + depth_count - 1, depth_count), me)
     greetings = 2 + len(near_peers) + len(outer_peers)
 
     inside = pl.ds(REACH, rows)
@@ -148,6 +151,53 @@
     for load in loads:
         load.start()
 
+    upper = lax.rem(here, 2) == 0
+
+    def by_core(if_upper, if_lower):
+        return jnp.where(upper, if_upper, if_lower)
+
+    far_low = by_core(0, rows - REACH)
+    most_low = by_core(REACH, 0)
+    most = rows - REACH
+    far_to = by_core(here - 1, here + 1)
+    near_to = by_core(here + 1, here - 1)
+    has_far = (far_to >= first) & (far_to <= last)
+
+    def halo_copy(field, number, moment, far, source=None):
+        if far:
+            start, target = by_core(REACH, rows), by_core(REACH + rows, 0)
+        else:
+            start, target = by_core(rows, REACH), by_core(0, REACH + rows)
+        if source is None:
+            source = field.at[moment, pl.ds(start, REACH), across]
+        else:
+            source = source.at[0, pl.ds(start - REACH, REACH)]
+        return pltpu.make_async_remote_copy(
+            src_ref=source,
+            dst_ref=field.at[moment, pl.ds(target, REACH), across],
+            send_sem=halo_send.at[number, moment, 1 if far else 0],
+            recv_sem=halo_recv.at[number, moment, 1 if far else 0],
+            device_id=(far_to if far else near_to, me),
+            device_id_type=MESH,
+        )
+
+    def when_far(far, body):
+        if far:
+            pl.when(has_far)(body)
+        else:
+            body()
+
+    def send_halo(field, number, moment, far, source=None):
+        when_far(far, lambda: halo_copy(field, number, moment, far, source).start())
+
+    def wait_halo(field, number, moment, far):
+        when_far(far, lambda: halo_copy(field, number, moment, far).wait_recv())
+
+    pl.semaphore_wait(barrier, greetings)
+
+    send_halo(wave, 0, 0, True, current_hbm)
+    send_halo(wave, 0, 0, False, current_hbm)
+
     pads = jnp.zeros((rows, PAD, lanes), jnp.float32)
     for field in (wave, scaled_adj):
         for moment in range(STEPS):
@@ -166,56 +216,6 @@
         for field in (wave, scaled_adj):
             for moment in range(STEPS):
                 field[moment, pl.ds(REACH + rows, REACH), across, :] = outside
-
-    def halo_copy(field, number, moment, up, source=None):
-        if source is None:
-            start = REACH if up else rows
-            source = field.at[moment, pl.ds(start, REACH), across]
-        target = field.at[moment, pl.ds(REACH + rows if up else 0, REACH), across]
-        side = 0 if up else 1
-        to = here - 1 if up else here + 1
-        return pltpu.make_async_remote_copy(
-            src_ref=source,
-            dst_ref=target,
-            send_sem=halo_send.at[number, moment, side],
-            recv_sem=halo_recv.at[number, moment, side],
-            device_id=(to, me),
-            device_id_type=MESH,
-        )
-
-    def send_halo(field, number, moment, up, source=None):
-        @pl.when(here > first if up else here < last)
-        def _():
-            halo_copy(field, number, moment, up, source).start()
-
-    def wait_halo(field, number, moment, above):
-        @pl.when(here > first if above else here < last)
-        def _():
-            halo_copy(field, number, moment, not above).wait_recv()
-
-    pl.semaphore_wait(barrier, greetings)
-
-    send_halo(wave, 0, 0, True, current_hbm.at[0, pl.ds(0, REACH)])
-    send_halo(wave, 0, 0, False, current_hbm.at[0, pl.ds(rows - REACH, REACH)])
-
-    loads[0].wait()
-    loads[1].wait()
-
-    def first_scaled(z):
-        scaled_adj[0, z + REACH, across, :] = courant[z] * adj[0, z]
-
-    def planes(low, high, body):
-        def one(z, carry):
-            body(z)
-            return carry
-
-        lax.fori_loop(low, high, one, 0)
-
-    planes(0, REACH, first_scaled)
-    send_halo(scaled_adj, 1, 0, True)
-    planes(rows - REACH, rows, first_scaled)
-    send_halo(scaled_adj, 1, 0, False)
-    planes(REACH, rows - REACH, first_scaled)
 
     lane_bits = lanes.bit_length() - 1
     for load in loads[6:]:
@@ -246,6 +246,25 @@
 
     lax.fori_loop(0, rows // 4, inject_block, 0)
 
+    loads[0].wait()
+    loads[1].wait()
+
+    def first_scaled(z):
+        scaled_adj[0, z + REACH, across, :] = courant[z] * adj[0, z]
+
+    def planes(low, count, body):
+        def one(number, carry):
+            for step in range(2):
+                body(low + 2 * number + step)
+            return carry
+
+        lax.fori_loop(0, count // 2, one, 0)
+
+    planes(far_low, REACH, first_scaled)
+    send_halo(scaled_adj, 1, 0, True)
+    planes(most_low, most, first_scaled)
+    send_halo(scaled_adj, 1, 0, False)
+
     source = source_ref[0]
     plane_ids = lax.broadcasted_iota(jnp.int32, (width, lanes), 0) * lanes
     plane_ids = plane_ids + lax.broadcasted_iota(jnp.int32, (width, lanes), 1)
@@ -303,7 +322,7 @@
                 total = total + adj[number, z] * lap[STEPS - number, z]
             terms[:, z] = total.reshape(shot_count, piece, lanes)
 
-    stretches = ((REACH, rows - 2 * REACH), (0, REACH), (rows - REACH, REACH))
+    stretches = ((most_low, most), (far_low, REACH))
 
     def part_copy(number, peer, slot):
         start, length = stretches[number]
@@ -317,27 +336,33 @@
         )
 
     def send_parts(number):
-        for step in range(1, shot_count):
+        for step in shot_order:
             part_copy(number, shot_peer(step), me).start()
 
-    def forward(moment, low, high):
-        for start in range(low, high, BLOCK):
-            along(wave, moment, start, BLOCK)
-        planes(low, high, functools.partial(forward_plane, moment))
-
-    def adjoint(moment, low, high):
-        for start in range(low, high, BLOCK):
-            along(scaled_adj, moment, start, BLOCK)
-        planes(low, high, functools.partial(adjoint_plane, moment))
+    def forward(moment, low, count):
+        for start in range(0, count, BLOCK):
+            along(wave, moment, low + start, BLOCK)
+        planes(low, count, functools.partial(forward_plane, moment))
+
+    def adjoint(moment, low, count):
+        for start in range(0, count, BLOCK):
+            along(scaled_adj, moment, low + start, BLOCK)
+        planes(low, count, functools.partial(adjoint_plane, moment))
 
     loads[2].wait()
     loads[3].wait()
     loads[4].wait()
     for moment in range(STEPS):
         more = moment < STEPS - 1
-        forward(moment, REACH, rows - REACH)
-        if not more:
-            adjoint(moment, REACH, rows - REACH)
+        wait_halo(wave, 0, moment, False)
+        forward(moment, most_low, most)
+        if more:
+            send_halo(wave, 0, moment + 1, False)
+        wait_halo(scaled_adj, 1, moment, False)
+        adjoint(moment, most_low, most)
+        if more:
+            send_halo(scaled_adj, 1, moment + 1, False)
+        else:
             send_parts(0)
         if moment == 0:
             loads[5].wait()
@@ -365,27 +390,15 @@
                     packed = jnp.where(row_lane == spot, value, packed)
             gram[...] = packed
         wait_halo(wave, 0, moment, True)
-        forward(moment, 0, REACH)
+        forward(moment, far_low, REACH)
         if more:
             send_halo(wave, 0, moment + 1, True)
-        wait_halo(wave, 0, moment, False)
-        forward(moment, rows - REACH, rows)
-        if more:
-            send_halo(wave, 0, moment + 1, False)
-        if more:
-            adjoint(moment, REACH, rows - REACH)
         wait_halo(scaled_adj, 1, moment, True)
-        adjoint(moment, 0, REACH)
+        adjoint(moment, far_low, REACH)
         if more:
             send_halo(scaled_adj, 1, moment + 1, True)
         else:
             send_parts(1)
-        wait_halo(scaled_adj, 1, moment, False)
-        adjoint(moment, rows - REACH, rows)
-        if more:
-            send_halo(scaled_adj, 1, moment + 1, False)
-        else:
-            send_parts(2)
 
     for number in range(len(stretches)):
         for step in range(1, shot_count):
@@ -397,15 +410,19 @@
         total = terms[me, z]
         for step in range(1, shot_count):
             total = total + parts[shot_peer(step), z]
+        pair_out[0, z] = total
         total = total * scale
-        gradient_out[z] = total
         return tuple(
             held + history[number // PAIRS, number % PAIRS, z] * total
             for number, held in enumerate(sums)
         )
 
     sums = lax.fori_loop(
-        0, rows, own_plane, tuple(jnp.zeros((piece, lanes), jnp.float32) for _ in range(2 * PAIRS))
+        0,
+        rows,
+        own_plane,
+        tuple(jnp.zeros((piece, lanes), jnp.float32) for _ in range(2 * PAIRS)),
+        unroll=4,
     )
     row_lane = lax.broadcasted_iota(jnp.int32, (1, lanes), 1)
     packed = gram[...]
@@ -484,17 +501,17 @@
     own_lateral = pl.ds(pl.multiple_of(me * piece, piece), piece)
 
     def direction_plane(z, carry):
-        search = gradient_out[z]
+        search = pair_out[0, z] * scale
         for i in range(PAIRS):
             search = search - alphas[i] * history[1, i, z]
         search = gamma * search
         for i in range(PAIRS):
             search = search + gains[i] * history[0, i, z]
-        direction_out[z] = -search
+        pair_out[1, z] = search
         next_piece[z] = courant[z, own_lateral, :] - 0.05 * search
         return carry
 
-    lax.fori_loop(0, rows, direction_plane, 0)
+    lax.fori_loop(0, rows, direction_plane, 0, unroll=4)
 
     def next_copy(peer, slot):
         spot = pl.ds(pl.multiple_of(slot * piece, piece), piece)
@@ -507,18 +524,15 @@
             device_id_type=MESH,
         )
 
-    for step in range(1, shot_count):
+    for step in shot_order:
         next_copy(shot_peer(step), me).start()
     own = pltpu.make_async_copy(next_piece, next_out.at[:, own_lateral], next_local)
     own.start()
 
     for number, field in enumerate((wave, scaled_adj)):
         for moment in range(STEPS):
-            for up in (True, False):
-
-                @pl.when(here > first if up else here < last)
-                def _():
-                    halo_copy(field, number, moment, up).wait_send()
+            when_far(True, halo_copy(field, number, moment, True).wait_send)
+            halo_copy(field, number, moment, False).wait_send()
 
     for number in range(len(stretches)):
         for step in range(1, shot_count):
@@ -554,15 +568,14 @@
     vmem = pl.BlockSpec(memory_space=pltpu.VMEM)
     anywhere = pl.BlockSpec(memory_space=pltpu.HBM)
     dma = pltpu.SemaphoreType.DMA
-    return pl.pallas_call(
+    pair, courant_next = pl.pallas_call(
         functools.partial(kernel, depth_count, shot_count, inner_count),
         out_shape=(
-            jax.ShapeDtypeStruct((rows, piece, lanes), f32),
-            jax.ShapeDtypeStruct((rows, piece, lanes), f32),
+            jax.ShapeDtypeStruct((2, rows, piece, lanes), f32),
             jax.ShapeDtypeStruct(slab, f32),
         ),
         in_specs=[pl.BlockSpec(memory_space=pltpu.SMEM)] + [anywhere] * 9,
-        out_specs=(vmem, vmem, anywhere),
+        out_specs=(vmem, anywhere),
         scratch_shapes=[
             pltpu.SMEM(wavelet.shape, f32),
             pltpu.VMEM(receiver_cell.shape, jnp.int32),
@@ -587,8 +600,8 @@
             dma((9,)),
             dma((2, STEPS, 2)),
             dma((2, STEPS, 2)),
-            dma((3, shot_count)),
-            dma((3, shot_count)),
+            dma((2, shot_count)),
+            dma((2, shot_count)),
             dma,
             dma,
             dma,
@@ -617,6 +630,7 @@
             )
         )
     )
+    return pair[0] * (1.0 / (shot_count * STEPS)), -pair[1], courant_next
 
 
 def solution(mesh):

time: 66.4 us -> 63.1 us (0.950)
  Pallas kernels: 63 us -> 60.3 us
  local copies, waits for them, and re-layouts: 2.05 us -> 0.79 us
    pallas_call x1, Pallas kernels: 63 us -> 60.3 us  [per_device(): pl.pallas_call(functools.partial(kernel, depth_count, shot_count, inner_c...]
    unnamed x3 -> x1, local copies, waits for them, and re-layouts: 2.05 us -> 0.79 us
where the time goes in v4:
time: 63.1 us; the launch traced here: 63 us
  Pallas kernels  60.3 us (96%)
  between operations  1.29 us (2%)
  local copies, waits for them, and re-layouts  0.79 us (1%)
  other arithmetic  0.66 us (1%)
    pallas_call x1, Pallas kernels, per_device(): pl.pallas_call(functools.partial(kernel, depth_count, shot_count, inner_c...  60.3 us

profile of v4, /device:TPU:1, one launch (start us, length us, event | category | flops | bytes accessed | tf_op | source)
XLA Modules:
  0.0 63.0 jit_solution(513796451817290811)
XLA Ops:
  1.3 60.3 %shard_map.121 = (f32[2,16,8,128]{3,2,1,0:T(8,128)S(1)}, f32[16,64,128]{2,1,0:T(8,128)S(1)}) custom-call(s32[1]{0:T(128)S(6)} %copy.14.source_ref, f32[1,4]{1,0:T(1,128)} %wavelet_hbm.1, s32[1,256]{1,0:T(1,128)} %receiver_hbm.1, f32[1,4,256]{2,1,0:T(4,128)} %residual_hbm.1, f32[16,64,128]{2,1,0:T(8,128)} %courant_hbm.1, f32[1,16,64,128]{3,2,1,0:T(8,128)} %before_hbm.1, ...), custom_call_target="tpu_custom_call" | custom-call | tf_op jit(solution)/shard_map/pallas_call | solution.py:571
  61.6 0.7 %negate_bitcast_fusion = (f32[16,8,128]{2,1,0:T(8,128)}, f32[16,8,128]{2,1,0:T(8,128)}) fusion(f32[2,16,8,128]{3,2,1,0:T(8,128)S(1)} %get-tuple-element.5), kind=kLoop, calls=%fused_computation | loop fusion | flops 32768 | bytes 262144 | tf_op jit(solution)/shard_map/neg | solution.py:633
  62.2 0.8 %copy.15 = f32[16,64,128]{2,1,0:T(8,128)} copy(f32[16,64,128]{2,1,0:T(8,128)S(1)} %get-tuple-element.14) | data formatting | bytes 1048576

commit v5 on v4

--- a/solution.py
+++ b/solution.py
@@ -364,31 +364,6 @@
             send_halo(scaled_adj, 1, moment + 1, False)
         else:
             send_parts(0)
-        if moment == 0:
-            loads[5].wait()
-            pairs = [(0, i, j) for j in range(PAIRS) for i in range(j + 1)]
-            pairs += [(1, i, j) for j in range(PAIRS) for i in range(j + 1)]
-
-            def gram_plane(z, sums):
-                held = [[history[kind, i, z] for i in range(PAIRS)] for kind in range(2)]
-                return tuple(
-                    total + held[kind][i] * held[1][j]
-                    for total, (kind, i, j) in zip(sums, pairs)
-                )
-
-            sums = lax.fori_loop(
-                0, rows, gram_plane, tuple(jnp.zeros((piece, lanes), jnp.float32) for _ in pairs)
-            )
-            row_lane = lax.broadcasted_iota(jnp.int32, (1, lanes), 1)
-            packed = jnp.zeros((1, lanes), jnp.float32)
-            for total, (kind, i, j) in zip(sums, pairs):
-                value = jnp.sum(jnp.sum(total, axis=0, keepdims=True), axis=1, keepdims=True)
-                spots = [(2 + PAIRS * kind + j) * 8 + i]
-                if kind == 1 and i != j:
-                    spots.append((2 + PAIRS * kind + i) * 8 + j)
-                for spot in spots:
-                    packed = jnp.where(row_lane == spot, value, packed)
-            gram[...] = packed
         wait_halo(wave, 0, moment, True)
         forward(moment, far_low, REACH)
         if more:
@@ -399,6 +374,31 @@
             send_halo(scaled_adj, 1, moment + 1, True)
         else:
             send_parts(1)
+
+    loads[5].wait()
+    pairs = [(0, i, j) for j in range(PAIRS) for i in range(j + 1)]
+    pairs += [(1, i, j) for j in range(PAIRS) for i in range(j + 1)]
+
+    def gram_plane(z, sums):
+        held = [[history[kind, i, z] for i in range(PAIRS)] for kind in range(2)]
+        return tuple(
+            total + held[kind][i] * held[1][j]
+            for total, (kind, i, j) in zip(sums, pairs)
+        )
+
+    sums = lax.fori_loop(
+        0, rows, gram_plane, tuple(jnp.zeros((piece, lanes), jnp.float32) for _ in pairs)
+    )
+    row_lane = lax.broadcasted_iota(jnp.int32, (1, lanes), 1)
+    packed = jnp.zeros((1, lanes), jnp.float32)
+    for total, (kind, i, j) in zip(sums, pairs):
+        value = jnp.sum(jnp.sum(total, axis=0, keepdims=True), axis=1, keepdims=True)
+        spots = [(2 + PAIRS * kind + j) * 8 + i]
+        if kind == 1 and i != j:
+            spots.append((2 + PAIRS * kind + i) * 8 + j)
+        for spot in spots:
+            packed = jnp.where(row_lane == spot, value, packed)
+    gram[...] = packed
 
     for number in range(len(stretches)):
         for step in range(1, shot_count):
@@ -455,12 +455,11 @@
         sums = [slots[slot] for slot in range(len(peers) + 1)]
         while len(sums) > 1:
             sums = [sums[i] + sums[i + 1] for i in range(0, len(sums), 2)]
-        every.wait_send()
-        return sums[0]
+        return sums[0], every
 
     near_me = me * inner_count + inner_me
-    packed = gather_sum(packed, slots_near, near_send, near_recv, near_me, near_peers)
-    packed = gather_sum(packed, slots_outer, outer_send, outer_recv, outer_me, outer_peers)
+    packed, near_every = gather_sum(packed, slots_near, near_send, near_recv, near_me, near_peers)
+    packed, outer_every = gather_sum(packed, slots_outer, outer_send, outer_recv, outer_me, outer_peers)
 
     spread = jnp.broadcast_to(packed, (8, lanes))
     sub = lax.broadcasted_iota(jnp.int32, (8, lanes), 0)
@@ -537,6 +536,8 @@
     for number in range(len(stretches)):
         for step in range(1, shot_count):
             part_copy(number, shot_peer(step), me).wait_send()
+    near_every.wait_send()
+    outer_every.wait_send()
     own.wait()
     for step in range(1, shot_count):
         next_copy(me, shot_peer(step)).wait_recv()

time: 63.1 us -> 62.9 us (level)
  no operation moved by 1% of the time
where the time goes in v5:
time: 62.9 us; the launch traced here: 62.8 us
  Pallas kernels  60 us (95%)
  between operations  1.29 us (2%)
  local copies, waits for them, and re-layouts  0.79 us (1%)
  other arithmetic  0.66 us (1%)
    pallas_call x1, Pallas kernels, per_device(): pl.pallas_call(functools.partial(kernel, depth_count, shot_count, inner_c...  60 us

profile of v5, /device:TPU:1, one launch (start us, length us, event | category | flops | bytes accessed | tf_op | source)
XLA Modules:
  0.0 62.8 jit_solution(10929821228707681995)
XLA Ops:
  1.3 60.0 %shard_map.121 = (f32[2,16,8,128]{3,2,1,0:T(8,128)S(1)}, f32[16,64,128]{2,1,0:T(8,128)S(1)}) custom-call(s32[1]{0:T(128)S(6)} %copy.14.source_ref, f32[1,4]{1,0:T(1,128)} %wavelet_hbm.1, s32[1,256]{1,0:T(1,128)} %receiver_hbm.1, f32[1,4,256]{2,1,0:T(4,128)} %residual_hbm.1, f32[16,64,128]{2,1,0:T(8,128)} %courant_hbm.1, f32[1,16,64,128]{3,2,1,0:T(8,128)} %before_hbm.1, ...), custom_call_target="tpu_custom_call" | custom-call | tf_op jit(solution)/shard_map/pallas_call | solution.py:572
  61.3 0.7 %negate_bitcast_fusion = (f32[16,8,128]{2,1,0:T(8,128)}, f32[16,8,128]{2,1,0:T(8,128)}) fusion(f32[2,16,8,128]{3,2,1,0:T(8,128)S(1)} %get-tuple-element.5), kind=kLoop, calls=%fused_computation | loop fusion | flops 32768 | bytes 262144 | tf_op jit(solution)/shard_map/neg | solution.py:634
  62.0 0.8 %copy.15 = f32[16,64,128]{2,1,0:T(8,128)} copy(f32[16,64,128]{2,1,0:T(8,128)S(1)} %get-tuple-element.14) | data formatting | bytes 1048576

commit v6 on v5

--- a/solution.py
+++ b/solution.py
@@ -254,11 +254,11 @@
 
     def planes(low, count, body):
         def one(number, carry):
-            for step in range(2):
-                body(low + 2 * number + step)
+            for step in range(BLOCK):
+                body(low + BLOCK * number + step)
             return carry
 
-        lax.fori_loop(0, count // 2, one, 0)
+        lax.fori_loop(0, count // BLOCK, one, 0)
 
     planes(far_low, REACH, first_scaled)
     send_halo(scaled_adj, 1, 0, True)

time: 62.9 us -> 63.1 us (level)
  no operation moved by 1% of the time
where the time goes in v6:
time: 63.1 us
  Pallas kernels  60.3 us (96%)
  between operations  1.29 us (2%)
  local copies, waits for them, and re-layouts  0.79 us (1%)
  other arithmetic  0.66 us (1%)
    pallas_call x1, Pallas kernels, per_device(): pl.pallas_call(functools.partial(kernel, depth_count, shot_count, inner_c...  60.3 us

profile of v6, /device:TPU:1, one launch (start us, length us, event | category | flops | bytes accessed | tf_op | source)
XLA Modules:
  0.0 63.1 jit_solution(7395349052012556447)
XLA Ops:
  1.3 60.3 %shard_map.121 = (f32[2,16,8,128]{3,2,1,0:T(8,128)S(1)}, f32[16,64,128]{2,1,0:T(8,128)S(1)}) custom-call(s32[1]{0:T(128)S(6)} %copy.14.source_ref, f32[1,4]{1,0:T(1,128)} %wavelet_hbm.1, s32[1,256]{1,0:T(1,128)} %receiver_hbm.1, f32[1,4,256]{2,1,0:T(4,128)} %residual_hbm.1, f32[16,64,128]{2,1,0:T(8,128)} %courant_hbm.1, f32[1,16,64,128]{3,2,1,0:T(8,128)} %before_hbm.1, ...), custom_call_target="tpu_custom_call" | custom-call | tf_op jit(solution)/shard_map/pallas_call | solution.py:572
  61.6 0.7 %negate_bitcast_fusion = (f32[16,8,128]{2,1,0:T(8,128)}, f32[16,8,128]{2,1,0:T(8,128)}) fusion(f32[2,16,8,128]{3,2,1,0:T(8,128)S(1)} %get-tuple-element.5), kind=kLoop, calls=%fused_computation | loop fusion | flops 32768 | bytes 262144 | tf_op jit(solution)/shard_map/neg | solution.py:634
  62.3 0.8 %copy.15 = f32[16,64,128]{2,1,0:T(8,128)} copy(f32[16,64,128]{2,1,0:T(8,128)S(1)} %get-tuple-element.14) | data formatting | bytes 1048576
